TPU v7x, 32 devices: a whole 2x2x4 slice. The times are simulated.
32 devices in a mesh: bins: 8 (over z, x), lat: 4 (over y, core).
Axes of the slice: x: 2, y: 2, z: 4, core: 2. Of those that a mesh axis runs over, the one named last changes fastest.
Arguments:
- spectrum: float32 [1152, 64, 384], P('bins', 'lat'), may hold values from 0.05 to 2
- sea_mask: int32 [64, 384], P('lat'), may hold values 0 or 1
- current: float32 [768, 128], P('bins', 'lat'), may hold values from -0.6 to 0.6
- partner_plus: int32 [1152], replicated, may hold values from 0 to 1151
- partner_minus: int32 [1152], replicated, may hold values from 0 to 1151
- source_map: int32 [768, 128], P('bins', 'lat'), may hold values from 0 to 8
Outputs:
- spectrum_out: float32 [1152, 64, 384], P('bins', 'lat')
- stokes: float32 [2, 64, 768, 128], P(None, None, 'bins', 'lat')
All inputs are finite; a program needn't handle non-finite values. No bound on the sum of `sea_mask` on one device may be relied on, other than what follows from the above.
Results may differ from a plain program's by a relative error of at most 0.000086.
Values sent between devices are 32-bit elements; how exact they have to be, the bound alone decides.
A program may use at most 128 MiB of HBM per device.

v0:
```python
import functools
import math

import jax
import jax.numpy as jnp
import numpy as np
from jax import lax
from jax.experimental import pallas as pl
from jax.experimental.pallas import tpu as pltpu
from jax.sharding import PartitionSpec as P

NDIR = 36
NFREQ = 32
LEV = 64


HIGHEST = lax.Precision.HIGHEST


def extended(block, sides, width):
    for axis, dim in sides:
        count = lax.axis_size(axis)
        forward = [(i, i + 1) for i in range(count - 1)]
        backward = [(target, source) for source, target in forward]
        low = lax.ppermute(
            lax.slice_in_dim(block, block.shape[dim] - width, None, axis=dim), axis, forward
        )
        high = lax.ppermute(lax.slice_in_dim(block, 0, width, axis=dim), axis, backward)
        block = jnp.concatenate([low, block, high], axis=dim)
    return block


def bin_tables():
    dir_index = jnp.arange(NDIR, dtype=jnp.float32)
    freq_index = jnp.arange(NFREQ, dtype=jnp.float32)
    angles = 2.0 * math.pi * (dir_index + 0.5) / NDIR
    speeds = 0.12 + 0.25 * (NFREQ - 1 - freq_index) / (NFREQ - 1)
    along_x = jnp.repeat(speeds, NDIR) * jnp.tile(jnp.cos(angles), NFREQ)
    along_y = jnp.repeat(speeds, NDIR) * jnp.tile(jnp.sin(angles), NFREQ)
    strength = jnp.repeat(0.06 * (1.0 + freq_index / (NFREQ - 1)), NDIR)
    levels = jnp.arange(LEV, dtype=jnp.float32) + 0.5
    wavenumber = 0.02 * jnp.power(1.15, freq_index)
    decay = jnp.repeat(jnp.exp(-levels[:, None] * wavenumber[None, :]), NDIR, axis=1)
    amplitude = 2.0 / math.sqrt(NDIR * NFREQ)
    cosines = jnp.tile(jnp.cos(angles), NFREQ)
    sines = jnp.tile(jnp.sin(angles), NFREQ)
    drift_table = amplitude * jnp.concatenate(
        [decay * cosines[None, :], decay * sines[None, :]], axis=0
    )
    return (along_x, along_y, strength, drift_table)


def fixed_tables():
    dir_index = np.arange(NDIR, dtype=np.float32)
    freq_index = np.arange(NFREQ, dtype=np.float32)
    angles = 2.0 * math.pi * (dir_index + 0.5) / NDIR
    speeds = 0.12 + 0.25 * (NFREQ - 1 - freq_index) / (NFREQ - 1)
    along_x = np.repeat(speeds, NDIR) * np.tile(np.cos(angles), NFREQ)
    along_y = np.repeat(speeds, NDIR) * np.tile(np.sin(angles), NFREQ)
    strength = np.repeat(0.06 * (1.0 + freq_index / (NFREQ - 1)), NDIR)
    levels = np.arange(LEV, dtype=np.float32) + 0.5
    wavenumber = 0.02 * np.power(np.float32(1.15), freq_index)
    decay = np.repeat(np.exp(-levels[:, None] * wavenumber[None, :]), NDIR, axis=1)
    amplitude = 2.0 / math.sqrt(NDIR * NFREQ)
    cosines = np.tile(np.cos(angles), NFREQ)
    sines = np.tile(np.sin(angles), NFREQ)
    drift_table = amplitude * np.concatenate(
        [decay * cosines[None, :], decay * sines[None, :]], axis=0
    )
    tables = (along_x, along_y, strength, drift_table)
    return tuple(np.asarray(table, dtype=np.float32) for table in tables)


def cell_means(current_cells):
    lon_count = current_cells.shape[0] // 2
    lat_count = current_cells.shape[1] // 2
    return current_cells.reshape(lon_count, 2, lat_count, 2).mean(axis=(1, 3))


def face_fluxes(padded, velocity, dimension):
    face_count = padded.shape[dimension] - 3

    def section(low_edge):
        return lax.slice_in_dim(padded, low_edge, low_edge + face_count, axis=dimension)

    left_value = (-section(0) + 5.0 * section(1) + 2.0 * section(2)) / 6.0
    right_value = (2.0 * section(1) + 5.0 * section(2) - section(3)) / 6.0
    return jnp.maximum(velocity, 0.0) * left_value + jnp.minimum(velocity, 0.0) * right_value


def transport(padded_rows, zonal_flow, along_x, along_y, sea_cells):
    row_count = padded_rows.shape[1] - 4
    spectra = padded_rows[:, 2 : 2 + row_count, :]
    padded_cols = jnp.pad(spectra, ((0, 0), (0, 0), (2, 2)))
    zonal_padded = jnp.pad(zonal_flow, ((0, 0), (1, 1)))
    face_zonal = 0.5 * (zonal_padded[:, :-1] + zonal_padded[:, 1:])
    speed_x = along_x[:, None, None] + face_zonal[None, :, :]
    flux_x = face_fluxes(padded_cols, speed_x, 2)
    flux_y = face_fluxes(padded_rows, along_y[:, None, None], 1)
    change = flux_x[:, :, 1:] - flux_x[:, :, :-1] + flux_y[:, 1:, :] - flux_y[:, :-1, :]
    return sea_cells[None, :, :] * (spectra - change)


def spread_to_ocean(rim, source_map):
    row_count = rim.shape[1] - 2
    col_count = rim.shape[2] - 2
    result = jnp.zeros((rim.shape[0], 2 * col_count, 2 * row_count), jnp.float32)
    for offset in range(9):
        row_shift = offset // 3 - 1
        col_shift = offset % 3 - 1
        shifted = rim[
            :, 1 + row_shift : 1 + row_shift + row_count, 1 + col_shift : 1 + col_shift + col_count
        ]
        shifted = jnp.swapaxes(shifted, 1, 2)
        shifted = jnp.repeat(jnp.repeat(shifted, 2, axis=1), 2, axis=2)
        result = result + jnp.where(source_map[None, :, :] == offset, shifted, jnp.float32(0.0))
    return result


def on_device_plain(spectrum, sea_mask, current, partner_plus, partner_minus, source_map):
    along_x, along_y, strength, drift_table = bin_tables()
    bin_count = NDIR * NFREQ
    local_bins = spectrum.shape[0]
    first_bin = lax.axis_index("bins") * local_bins
    local_x = lax.dynamic_slice_in_dim(along_x, first_bin, local_bins)
    local_y = lax.dynamic_slice_in_dim(along_y, first_bin, local_bins)
    sea_cells = sea_mask.astype(jnp.float32)
    strip_flow = cell_means(current)
    zonal_flow = lax.all_gather(strip_flow, "bins", axis=0, tiled=True).T
    masked = spectrum * sea_cells[None, :, :]
    padded = extended(masked, (("lat", 1),), 2)
    after_first = transport(padded, zonal_flow, local_x, local_y, sea_cells)
    bin_ids = jnp.arange(bin_count, dtype=jnp.int32)
    plus_table = (partner_plus[:, None] == bin_ids[None, :]).astype(jnp.float32)
    minus_table = (partner_minus[:, None] == bin_ids[None, :]).astype(jnp.float32)
    contract_first = (((0,), (0,)), ((), ()))
    arrived = lax.all_to_all(after_first, "bins", split_axis=2, concat_axis=0, tiled=True)
    row_count = arrived.shape[1]
    col_count = arrived.shape[2]
    flat_rows = arrived.reshape(bin_count, row_count * col_count)
    plus_part = jnp.dot(plus_table, flat_rows, precision=HIGHEST)
    minus_part = jnp.dot(minus_table, flat_rows, precision=HIGHEST)
    source = strength[:, None] * (
        flat_rows * flat_rows * (plus_part + minus_part) - 2.0 * flat_rows * plus_part * minus_part
    )
    back = lax.dot_general(plus_table, source, contract_first, precision=HIGHEST) + lax.dot_general(
        minus_table, source, contract_first, precision=HIGHEST
    )
    middle = flat_rows + (source - 0.5 * back)
    drift_rows = jnp.dot(drift_table, middle, precision=HIGHEST)
    middle, drift_rows = (
        middle.reshape(bin_count, row_count, col_count),
        drift_rows.reshape(2 * LEV, row_count, col_count),
    )
    rim = extended(drift_rows, (("bins", 2), ("lat", 1)), 1)
    ocean = spread_to_ocean(rim, source_map)
    stokes = ocean.reshape(2, LEV, ocean.shape[1], ocean.shape[2])
    returned = lax.all_to_all(middle, "bins", split_axis=0, concat_axis=2, tiled=True)
    padded_again = extended(returned, (("lat", 1),), 2)
    second = transport(padded_again, zonal_flow, local_x, local_y, sea_cells)
    return (second, stokes)


MESH = pl.DeviceIdType.MESH
TILE = 128
EDGE = 8
VMEM = pltpu.VMEM


def enter(count, me):
    barrier = pltpu.get_barrier_semaphore()
    for step in range(1, count):
        pl.semaphore_signal(
            barrier,
            inc=1,
            device_id={"bins": lax.rem(me + step, count)},
            device_id_type=MESH,
        )
    pl.semaphore_wait(barrier, count - 1)


def enter_all(count, me, band, bands):
    barrier = pltpu.get_barrier_semaphore()
    for step in range(1, count):
        pl.semaphore_signal(
            barrier,
            inc=1,
            device_id={"bins": lax.rem(me + step, count)},
            device_id_type=MESH,
        )
    for step in (1, bands - 1):
        pl.semaphore_signal(
            barrier,
            inc=1,
            device_id={"lat": lax.rem(band + step, bands)},
            device_id_type=MESH,
        )
    pl.semaphore_wait(barrier, count + 1)


def gather_kernel(count, strip_ref, out_ref, send_sem, recv_sem):
    me = lax.axis_index("bins")
    enter(count, me)
    copies = []
    for step in range(1, count):
        copy = pltpu.make_async_remote_copy(
            src_ref=strip_ref,
            dst_ref=out_ref.at[me],
            send_sem=send_sem.at[step],
            recv_sem=recv_sem.at[step],
            device_id={"bins": lax.rem(me + step, count)},
            device_id_type=MESH,
        )
        copy.start()
        copies.append(copy)
    own = pltpu.make_async_copy(strip_ref, out_ref.at[me], send_sem.at[0])
    own.start()
    own.wait()
    for copy in copies:
        copy.wait()


def gather_strips(strip, count):
    return pl.pallas_call(
        functools.partial(gather_kernel, count),
        out_shape=jax.ShapeDtypeStruct((count,) + strip.shape, strip.dtype),
        in_specs=[pl.BlockSpec(memory_space=VMEM)],
        out_specs=pl.BlockSpec(memory_space=VMEM),
        scratch_shapes=[
            pltpu.SemaphoreType.DMA((count,)),
            pltpu.SemaphoreType.DMA((count,)),
        ],
        compiler_params=pltpu.CompilerParams(collective_id=0, has_side_effects=True),
    )(strip)


def transport_kernel(
    bins_first, x_ref, low_ref, high_ref, mask_ref, half_ref, coef_ref, edge_ref, out_ref
):
    rows = mask_ref.shape[0]
    cols = mask_ref.shape[1]
    blocks = coef_ref.shape[0] // 8
    lane = lax.broadcasted_iota(jnp.int32, (8, cols), 1)
    at_first = lane == 0
    at_second = lane <= 1
    at_last = lane == cols - 1
    half = half_ref[...]
    half_low = jnp.where(
        lax.broadcasted_iota(jnp.int32, half.shape, 1) == 0, 0.0, pltpu.roll(half, 1, 1)
    )
    sixth = jnp.float32(1.0 / 6.0)

    def block_step(block, carry):
        at = pl.multiple_of(block * 8, 8)
        here = pl.ds(at, 8)
        mask = mask_ref[...]
        low = [edge_ref[0:1, :] * low_ref[row, here, :] for row in range(2)]
        high = [edge_ref[1:2, :] * high_ref[row, here, :] for row in range(2)]
        if bins_first:
            turned = pltpu.einshape("brl->rbl", x_ref[here, :, :] * mask[None])
            inner = [turned[row] for row in range(rows)]
        else:
            inner = [x_ref[row, here, :] for row in range(rows)]
        f = low + inner + high
        coefs = coef_ref[here, :]
        coef = [jnp.broadcast_to(coefs[:, i : i + 1], (8, cols)) for i in range(6)]
        results = []
        for row in range(rows):
            c = f[row + 2]
            m1 = jnp.where(at_first, 0.0, pltpu.roll(c, 1, 1))
            m2 = jnp.where(at_second, 0.0, pltpu.roll(c, 2, 1))
            p1 = jnp.where(at_last, 0.0, pltpu.roll(c, cols - 1, 1))
            own_half = half[row : row + 1, :]
            speed = coef[0] + (own_half + half_low[row : row + 1, :])
            ahead = speed > 0.0
            part = 3.0 * jnp.where(ahead, m1, c) - jnp.where(ahead, m2, p1)
            flux = (speed * sixth) * (part + 2.0 * (m1 + c))
            end_speed = coef[0] + own_half
            end = (end_speed * sixth) * jnp.where(end_speed > 0.0, 5.0 * c - m1, 2.0 * c)
            upper = jnp.where(at_last, end, pltpu.roll(flux, cols - 1, 1))
            along_y = (
                coef[1] * f[row]
                + coef[2] * f[row + 1]
                + coef[3] * c
                + coef[4] * f[row + 3]
                + coef[5] * f[row + 4]
            )
            results.append(mask[row : row + 1, :] * (c - ((upper - flux) + along_y)))
        if bins_first:
            for row in range(rows):
                out_ref[row, here, :] = results[row]
        else:
            out_ref[here, :, :] = pltpu.einshape("rbl->brl", jnp.stack(results))
        return carry

    lax.fori_loop(0, blocks, block_step, 0)


def transport_call(x, low, high, sea_cells, half, coefs, edges, bins_first):
    rows, cols = sea_cells.shape
    bins = coefs.shape[0]
    group = bins // 3 if bins % 24 == 0 else bins
    by_bin = pl.BlockSpec((group, rows, cols), lambda i: (i, 0, 0))
    by_row = pl.BlockSpec((rows, group, cols), lambda i: (0, i, 0))
    edge = pl.BlockSpec((2, group, cols), lambda i: (0, i, 0))
    full = pl.BlockSpec((rows, cols), lambda i: (0, 0))
    return pl.pallas_call(
        functools.partial(transport_kernel, bins_first),
        grid=(bins // group,),
        out_shape=jax.ShapeDtypeStruct(
            (rows, bins, cols) if bins_first else (bins, rows, cols), jnp.float32
        ),
        in_specs=[
            by_bin if bins_first else by_row,
            edge,
            edge,
            full,
            full,
            pl.BlockSpec((group, 8), lambda i: (i, 0)),
            pl.BlockSpec((2, cols), lambda i: (0, 0)),
        ],
        out_specs=by_row if bins_first else by_bin,
    )(x, low, high, sea_cells, half, coefs, edges)


def halves(value):
    high = value.astype(jnp.bfloat16)
    return high, (value - high.astype(jnp.float32)).astype(jnp.bfloat16)


def middle_kernel(
    count,
    bands,
    x_ref,
    plus_col_ref,
    minus_col_ref,
    plus_row_ref,
    minus_row_ref,
    strength_ref,
    drift_ref,
    index_ref,
    out_ref,
    low_ref,
    high_ref,
    stokes_ref,
    arrived,
    middle,
    plus_table,
    minus_table,
    back_table,
    high,
    low,
    source_high,
    source_low,
    total,
    profile,
    near,
    ocean,
    in_send,
    in_recv,
    back_send,
    back_recv,
    near_send,
    near_recv,
    edge_send,
    edge_recv,
    ocean_sem,
):
    me = lax.axis_index("bins")
    band = lax.axis_index("lat")
    enter_all(count, me, band, bands)
    each = arrived.shape[0]
    bins = arrived.shape[1]
    cols = arrived.shape[2]
    local = bins // count
    tiles = bins // TILE
    own_cols = cols // count
    mine = pl.ds(pl.multiple_of(me * local, 8), local)

    def send(src, dst, send_sem, recv_sem, peer, axis="bins"):
        copy = pltpu.make_async_remote_copy(
            src_ref=src,
            dst_ref=dst,
            send_sem=send_sem,
            recv_sem=recv_sem,
            device_id={axis: peer},
            device_id_type=MESH,
        )
        copy.start()
        return copy

    incoming = []
    for r in range(each):
        group = []
        for step in range(1, count):
            peer = lax.rem(me + step, count)
            group.append(
                send(
                    x_ref.at[r * count + peer],
                    arrived.at[r, mine, :],
                    in_send.at[r, step],
                    in_recv.at[r, step],
                    peer,
                )
            )
        own = pltpu.make_async_copy(
            x_ref.at[r * count + me], arrived.at[r, mine, :], in_send.at[r, 0]
        )
        own.start()
        group.append(own)
        incoming.append(group)

    def table_step(tile, carry):
        here = pl.ds(pl.multiple_of(tile * TILE, TILE), TILE)
        along = lax.broadcasted_iota(jnp.int32, (TILE, bins), 1)
        down = lax.broadcasted_iota(jnp.int32, (TILE, bins), 0) + tile * TILE
        one = jnp.float32(1.0)
        zero = jnp.float32(0.0)
        plus_table[here, :] = jnp.where(plus_col_ref[here, :] == along, one, zero).astype(
            jnp.bfloat16
        )
        minus_table[here, :] = jnp.where(minus_col_ref[here, :] == along, one, zero).astype(
            jnp.bfloat16
        )
        back_table[here, :] = (
            jnp.where(plus_row_ref[...] == down, one, zero)
            + jnp.where(minus_row_ref[...] == down, one, zero)
        ).astype(jnp.bfloat16)
        return carry

    lax.fori_loop(0, tiles, table_step, 0)
    profile[...] = jnp.zeros_like(profile)

    outgoing = []
    nearby = []
    width = own_cols + 2 * EDGE
    for r in range(each):
        for copy in incoming[r]:
            copy.wait()

        def split_step(tile, carry):
            here = pl.ds(pl.multiple_of(tile * TILE, TILE), TILE)
            high[here, :], low[here, :] = halves(arrived[r, here, :])
            return carry

        lax.fori_loop(0, tiles, split_step, 0)

        def pick(table, here, upper, lower):
            rows = table[here, :]
            return jnp.dot(rows, upper[...], preferred_element_type=jnp.float32) + jnp.dot(
                rows, lower[...], preferred_element_type=jnp.float32
            )

        def source_step(tile, carry):
            here = pl.ds(pl.multiple_of(tile * TILE, TILE), TILE)
            plus = pick(plus_table, here, high, low)
            minus = pick(minus_table, here, high, low)
            own_rows = arrived[r, here, :]
            source = strength_ref[here, :] * (
                own_rows * own_rows * (plus + minus) - 2.0 * own_rows * plus * minus
            )
            source_high[here, :], source_low[here, :] = halves(source)
            middle[r, here, :] = own_rows + source
            return carry

        lax.fori_loop(0, tiles, source_step, 0)
        total[...] = jnp.zeros_like(total)

        def back_step(tile, carry):
            here = pl.ds(pl.multiple_of(tile * TILE, TILE), TILE)
            rows = middle[r, here, :] - 0.5 * pick(back_table, here, source_high, source_low)
            middle[r, here, :] = rows
            total[...] += jnp.dot(
                drift_ref[:, here], rows, precision=HIGHEST, preferred_element_type=jnp.float32
            )
            return carry

        lax.fori_loop(0, tiles, back_step, 0)
        profile[r, pl.ds(EDGE, cols), :] = total[...].T
        for step in range(count):
            peer = lax.rem(me + step, count)
            src = profile.at[r, pl.ds(pl.multiple_of(peer * own_cols, 8), width), :]
            dst = near.at[2 + r * count + me]
            if step == 0:
                copy = pltpu.make_async_copy(src, dst, near_send.at[r, 0])
                copy.start()
            else:
                copy = send(src, dst, near_send.at[r, step], near_recv.at[r, step], peer)
            nearby.append(copy)
        group = []
        for step in range(1, count):
            peer = lax.rem(me + step, count)
            group.append(
                send(
                    middle.at[r, pl.ds(pl.multiple_of(peer * local, 8), local), :],
                    out_ref.at[r * count + me],
                    back_send.at[r, step],
                    back_recv.at[r, step],
                    peer,
                )
            )
        own = pltpu.make_async_copy(
            middle.at[r, mine, :], out_ref.at[r * count + me], back_send.at[r, 0]
        )
        own.start()
        group.append(own)
        outgoing.append(group)

    rows = each * count
    below = lax.rem(band + bands - 1, bands)
    above = lax.rem(band + 1, bands)
    edge_copies = []

    def send_edge(src, dst, slot, peer):
        edge_copies.append(send(src, dst, edge_send.at[slot], edge_recv.at[slot], peer, "lat"))

    for copy in outgoing[0]:
        copy.wait()
    send_edge(out_ref.at[pl.ds(0, 2)], high_ref, 0, below)
    for copy in nearby:
        copy.wait()
    send_edge(near.at[pl.ds(2, 2)], near.at[pl.ds(rows + 2, 2)], 1, below)
    send_edge(near.at[pl.ds(rows, 2)], near.at[pl.ds(0, 2)], 2, above)
    edge_copies[1].wait()
    edge_copies[2].wait()
    near[pl.ds(0, 2)] = near[pl.ds(0, 2)] * jnp.where(band == 0, 0.0, 1.0)
    near[pl.ds(rows + 2, 2)] = near[pl.ds(rows + 2, 2)] * jnp.where(band == bands - 1, 0.0, 1.0)

    ocean_copies = []
    depth = (rows + 4) * 16
    profiles = near.shape[2]
    lats = 2 * rows
    across = TILE // lats
    for octet in range(ocean.shape[1] // 8):
        strips = []
        for pair in range(octet * 8 // across, (octet + 1) * 8 // across):
            base = (EDGE - 1 + pair * across // 2) // 8 * 8
            window = near[:, base : base + 16, :].reshape(depth, profiles)
            chosen = (
                lax.broadcasted_iota(jnp.int32, (depth, TILE), 0) == index_ref[pair : pair + 1, :]
            )
            found = lax.dot_general(
                window,
                jnp.where(chosen, jnp.float32(1.0), jnp.float32(0.0)),
                (((0,), (0,)), ((), ())),
                precision=HIGHEST,
                preferred_element_type=jnp.float32,
            )
            strips += [found[:, i * lats : (i + 1) * lats] for i in range(across)]
        here = pl.ds(octet * 8, 8)
        ocean[:, here, :] = pltpu.einshape("xcl->cxl", jnp.stack(strips))
        copy = pltpu.make_async_copy(
            ocean.at[:, here, :], stokes_ref.at[:, here, :], ocean_sem.at[octet]
        )
        copy.start()
        ocean_copies.append(copy)

    for group in outgoing[1:]:
        for copy in group:
            copy.wait()
    send_edge(out_ref.at[pl.ds(rows - 2, 2)], low_ref, 3, above)
    edge_copies[0].wait()
    edge_copies[3].wait()
    for copy in ocean_copies:
        copy.wait()


def middle_call(x, partner_plus, partner_minus, strength, drift_table, source_map, count, bands):
    rows, local, cols = x.shape
    bins = local * count
    each = rows // count
    profiles = drift_table.shape[0]
    width = cols // count + 2 * EDGE
    lons, lats = source_map.shape
    lon = np.arange(lons, dtype=np.int32)[:, None]
    lat = np.arange(lats, dtype=np.int32)[None, :]
    across = TILE // lats
    base = (EDGE - 1 + lon // across * across // 2) // 8 * 8
    index = (lat // 2 + source_map // 3 + 1) * 16 + (
        EDGE - 1 + lon // 2 - base + source_map % 3
    )
    edge = jax.ShapeDtypeStruct((2, local, cols), jnp.float32)
    vmem = pl.BlockSpec(memory_space=VMEM)
    hbm = pl.BlockSpec(memory_space=pl.ANY)
    return pl.pallas_call(
        functools.partial(middle_kernel, count, bands),
        out_shape=(
            jax.ShapeDtypeStruct(x.shape, jnp.float32),
            edge,
            edge,
            jax.ShapeDtypeStruct((profiles, lons, lats), jnp.float32),
        ),
        in_specs=[hbm] + [vmem] * 7,
        out_specs=(hbm,) * 4,
        scratch_shapes=[
            VMEM((each, bins, cols), jnp.float32),
            VMEM((each, bins, cols), jnp.float32),
            VMEM((bins, bins), jnp.bfloat16),
            VMEM((bins, bins), jnp.bfloat16),
            VMEM((bins, bins), jnp.bfloat16),
            VMEM((bins, cols), jnp.bfloat16),
            VMEM((bins, cols), jnp.bfloat16),
            VMEM((bins, cols), jnp.bfloat16),
            VMEM((bins, cols), jnp.bfloat16),
            VMEM((profiles, cols), jnp.float32),
            VMEM((each, cols + 2 * EDGE, profiles), jnp.float32),
            VMEM((rows + 4, width, profiles), jnp.float32),
            VMEM((profiles, lons, lats), jnp.float32),
            pltpu.SemaphoreType.DMA((each, count)),
            pltpu.SemaphoreType.DMA((each, count)),
            pltpu.SemaphoreType.DMA((each, count)),
            pltpu.SemaphoreType.DMA((each, count)),
            pltpu.SemaphoreType.DMA((each, count)),
            pltpu.SemaphoreType.DMA((each, count)),
            pltpu.SemaphoreType.DMA((4,)),
            pltpu.SemaphoreType.DMA((4,)),
            pltpu.SemaphoreType.DMA((lons // 8,)),
        ],
        compiler_params=pltpu.CompilerParams(
            collective_id=1, has_side_effects=True, vmem_limit_bytes=56 * 1024 * 1024
        ),
    )(
        x,
        partner_plus[:, None],
        partner_minus[:, None],
        partner_plus[None, :],
        partner_minus[None, :],
        strength[:, None],
        drift_table,
        index.reshape(lons * lats // TILE, TILE),
    )


def exchange_rows(low_side, high_side):
    count = lax.axis_size("lat")
    forward = [(i, i + 1) for i in range(count - 1)]
    backward = [(target, source) for source, target in forward]
    return lax.ppermute(high_side, "lat", forward), lax.ppermute(low_side, "lat", backward)


def on_device_fast(spectrum, sea_mask, current, partner_plus, partner_minus, source_map):
    count = lax.axis_size("bins")
    bands = lax.axis_size("lat")
    band = lax.axis_index("lat")
    along_x, along_y, strength, drift_table = fixed_tables()
    local_bins, row_count, col_count = spectrum.shape
    forth = np.maximum(along_y, 0.0) / 6.0
    back = np.minimum(along_y, 0.0) / 6.0
    zeros = np.zeros_like(forth)
    coefs = np.stack(
        [
            along_x,
            forth,
            -6.0 * forth - 2.0 * back,
            3.0 * forth - 3.0 * back,
            2.0 * forth + 6.0 * back,
            -back,
            zeros,
            zeros,
        ],
        axis=1,
    )
    coefs = lax.dynamic_slice_in_dim(jnp.asarray(coefs, jnp.float32), lax.axis_index("bins") * local_bins, local_bins)
    sea_cells = sea_mask.astype(jnp.float32)
    strip = 0.5 * cell_means(current).T
    strip_cols = strip.shape[1]
    low_side = jnp.swapaxes(spectrum[:, :2, :] * sea_cells[None, :2, :], 0, 1)
    high_side = jnp.swapaxes(spectrum[:, -2:, :] * sea_cells[None, -2:, :], 0, 1)
    low, high = exchange_rows(low_side, high_side)
    strips = gather_strips(jnp.pad(strip, ((0, 0), (0, TILE - strip_cols))), count)
    half = jnp.swapaxes(strips[:, :, :strip_cols], 0, 1).reshape(row_count, col_count)
    ones = jnp.ones((2, col_count), jnp.float32)
    first = transport_call(spectrum, low, high, sea_cells, half, coefs, ones, True)
    middle, low, high, stokes = middle_call(
        first, partner_plus, partner_minus, strength, drift_table, source_map, count, bands
    )
    inside = jnp.stack([band > 0, band < bands - 1]).astype(jnp.float32)
    edges = jnp.broadcast_to(inside[:, None], (2, col_count))
    second = transport_call(middle, low, high, sea_cells, half, coefs, edges, False)
    return (second, stokes.reshape(2, LEV, *source_map.shape))


def on_device(spectrum, sea_mask, current, partner_plus, partner_minus, source_map):
    count = lax.axis_size("bins")
    bins, rows, cols = spectrum.shape
    bands = lax.axis_size("lat")
    lons, lats = source_map.shape
    fits = (
        rows % count == 0
        and rows % 8 == 0
        and bins % 8 == 0
        and cols % TILE == 0
        and cols // count % 8 == 0
        and cols // count <= TILE
        and bins * count % TILE == 0
        and 4 * lats == TILE
        and lats == 2 * rows
        and lons % 8 == 0
        and count > 1
        and bands > 1
    )
    body = on_device_fast if fits else on_device_plain
    return body(spectrum, sea_mask, current, partner_plus, partner_minus, source_map)


def solution(mesh):
    return jax.shard_map(
        on_device,
        mesh=mesh,
        in_specs=(
            P("bins", "lat", None),
            P("lat", None),
            P("bins", "lat"),
            P(),
            P(),
            P("bins", "lat"),
        ),
        out_specs=(P("bins", "lat", None), P(None, None, "bins", "lat")),
        check_vma=False,
    )
```

profile of v0, /device:TPU:9, one launch (start us, length us, event | category | flops | bytes accessed | tf_op | source)
XLA Modules:
  0.0 237.1 jit_solution(5024775188084931073)
XLA Ops:
  0.6 0.0 copy-start.7
  0.6 0.0 copy-start.8
  0.7 0.8 convert_element_type.12.mask_ref
  1.5 2.3 fusion.8
  3.8 3.7 %collective-permute-start = (f32[2,144,384]{2,1,0:T(8,128)S(1)}, f32[2,144,384]{2,1,0:T(8,128)S(1)}, u32[]{:S(2)}, u32[]{:S(2)}) collective-permute-start(f32[2,144,384]{2,1,0:T(8,128)S(1)} %fusion.1), channel_id=1, source_target_pairs={{0,1},{1,2},{2,3},{4,5},{5,6},{6,7},{8,9},{9,10},{10,11},{12,13},{... | collective-permute-start | bytes 1327112 | tf_op jit(solution)/shard_map/ppermute | solution.py:638
  7.6 1.9 collective-permute-start.1
  9.5 0.0 copy-done.3
  9.5 1.0 broadcast_in_dim.29.plus_col_ref
  10.6 0.6 broadcast_in_dim.26.plus_row_ref
  11.2 1.0 broadcast_in_dim.30.minus_col_ref
  12.2 0.6 broadcast_in_dim.27.minus_row_ref
  12.8 0.4 reshape.35
  13.2 0.2 reduce_sum.9
  13.4 0.6 pad.4.strip_ref
  14.0 6.9 %shard_map.122 = f32[8,16,128]{2,1,0:T(8,128)} custom-call(f32[16,128]{1,0:T(8,128)} %pad.4.strip_ref), custom_call_target="tpu_custom_call" | custom-call | tf_op jit(solution)/shard_map/pallas_call | solution.py:224
  20.9 0.8 slice_bitcast_fusion
  21.8 0.7 reshape.36.half_ref
  22.5 0.1 fusion.5
  22.5 0.1 copy.21
  22.6 0.7 reshape.37.index_ref
  23.3 0.1 add_convert_fusion
  23.4 1.5 constant_dynamic-slice_fusion.coef_ref
  24.9 0.0 collective-permute-done.low_ref
  24.9 0.0 collective-permute-done.1.high_ref
  24.9 0.7 broadcast_in_dim.23.edge_ref
  25.6 0.1 copy-done
  25.7 0.2 copy-done.1
  25.9 14.1 %shard_map.123.x_ref = f32[16,144,384]{2,1,0:T(8,128)} custom-call(f32[144,16,384]{2,1,0:T(8,128)} %x_ref.1, f32[2,144,384]{2,1,0:T(8,128)} %copy-done, f32[2,144,384]{2,1,0:T(8,128)} %copy-done.1, f32[16,384]{1,0:T(8,128)} %copy-done.2, f32[16,384]{1,0:T(8,128)} %reshape.36.half_ref, f32[144,8]{1,0:T(8,128)} %constant_dynamic-slice_fusion.coef_ref, ...), custom_call_target="tpu_custom_call" | custom-call | tf_op jit(solution)/shard_map/pallas_call | solution.py:307
  39.9 175.2 %shard_map.124 = (f32[16,144,384]{2,1,0:T(8,128)}, f32[2,144,384]{2,1,0:T(8,128)}, f32[2,144,384]{2,1,0:T(8,128)}, f32[128,96,32]{2,1,0:T(8,128)}) custom-call(f32[16,144,384]{2,1,0:T(8,128)} %shard_map.123.x_ref, s32[1152,1]{1,0:T(8,128)} %broadcast_in_dim.29.plus_col_ref, s32[1152,1]{1,0:T(8,128)} %broadcast_in_dim.30.minus_col_ref, ...), custom_call_target="tpu_custom_call" | custom-call | tf_op jit(solution)/shard_map/pallas_call | solution.py:585
  215.1 5.8 %copy.24 = f32[2,64,96,32]{2,3,1,0:T(8,128)} copy(f32[2,64,96,32]{3,2,1,0:T(8,128)} %bitcast.13) | data formatting | bytes 3145728
  220.9 0.7 broadcast_in_dim.28.edge_ref
  221.5 15.6 %shard_map.125 = f32[144,16,384]{2,1,0:T(8,128)} custom-call(f32[16,144,384]{2,1,0:T(8,128)} %get-tuple-element.6.x_ref, f32[2,144,384]{2,1,0:T(8,128)} %get-tuple-element.7.low_ref, f32[2,144,384]{2,1,0:T(8,128)} %get-tuple-element.8.high_ref, f32[16,384]{1,0:T(8,128)} %copy-done.2, f32[16,384]{1,0:T(8,128)} %reshape.36.half_ref, ...), custom_call_target="tpu_custom_call" | custom-call | tf_op jit(solution)/shard_map/pallas_call | solution.py:307
  (18 shorter events, 0.1 us)
Async XLA Ops:
  0.6 21.8 %copy-start.7 = (s32[32]{0:T(128)S(1)}, s32[32]{0:T(128)}, u32[]{:S(2)}) copy-start(s32[32]{0:T(128)} %constant.64) | copy-start | bytes 388
  0.6 21.8 %copy-start.8 = (s32[96]{0:T(128)S(1)}, s32[96]{0:T(128)}, u32[]{:S(2)}) copy-start(s32[96]{0:T(128)} %constant.65) | copy-start | bytes 1156
  0.7 8.9 %copy-start.3 = (s32[1152]{0:T(1024)S(1)}, s32[1152]{0:T(1024)}, u32[]{:S(2)}) copy-start(s32[1152]{0:T(1024)} %param.14) | copy-start | bytes 13828
  0.7 10.5 %copy-start.4 = (s32[1152]{0:T(1024)S(1)}, s32[1152]{0:T(1024)}, u32[]{:S(2)}) copy-start(s32[1152]{0:T(1024)} %param.15) | copy-start | bytes 13828
  0.7 12.1 %copy-start.5 = (f32[96,32]{0,1:T(8,128)S(1)}, f32[96,32]{0,1:T(8,128)}, u32[]{:S(2)}) copy-start(f32[96,32]{0,1:T(8,128)} %param.13) | copy-start | bytes 36868
  0.7 21.8 %copy-start.6 = (s32[96,32]{0,1:T(8,128)S(1)}, s32[96,32]{0,1:T(8,128)}, u32[]{:S(2)}) copy-start(s32[96,32]{0,1:T(8,128)} %param.16) | copy-start | bytes 36868
  1.5 23.5 %copy-start.2 = (f32[16,384]{1,0:T(8,128)}, f32[16,384]{1,0:T(8,128)S(1)}, u32[]{:S(2)}) copy-start(f32[16,384]{1,0:T(8,128)S(1)} %convert_element_type.12.mask_ref) | copy-start | bytes 73732
  3.8 21.1 %collective-permute-start = (f32[2,144,384]{2,1,0:T(8,128)S(1)}, f32[2,144,384]{2,1,0:T(8,128)S(1)}, u32[]{:S(2)}, u32[]{:S(2)}) collective-permute-start(f32[2,144,384]{2,1,0:T(8,128)S(1)} %fusion.1), channel_id=1, source_target_pairs={{0,1},{1,2},{2,3},{4,5},{5,6},{6,7},{8,9},{9,10},{10,11},{12,13},{... | collective-permute-start | bytes 1327112 | tf_op jit(solution)/shard_map/ppermute | solution.py:638
  7.6 17.3 %collective-permute-start.1 = (f32[2,144,384]{2,1,0:T(8,128)S(1)}, f32[2,144,384]{2,1,0:T(8,128)S(1)}, u32[]{:S(2)}, u32[]{:S(2)}) collective-permute-start(f32[2,144,384]{2,1,0:T(8,128)S(1)} %fusion), channel_id=1, source_target_pairs={{1,0},{2,1},{3,2},{5,4},{6,5},{7,6},{9,8},{10,9},{11,10},{13,12},{... | collective-permute-start | bytes 1327112 | tf_op jit(solution)/shard_map/ppermute | solution.py:638
  24.9 0.8 copy-start
  24.9 0.9 copy-start.1
where the time goes:
time: 240 us; the launch traced here: 237 us
  Pallas kernels  212 us (88%)
  local copies, waits for them, and re-layouts  17.7 us (7%)
  starting transfers between devices  5.63 us (2%)
    pallas_call x1, Pallas kernels, middle_call(): pl.pallas_call(functools.partial(middle_kernel, count, bands), out_shape=...  175 us
    pallas_call x2, Pallas kernels, transport_call(): pl.pallas_call(functools.partial(transport_kernel, bins_first), grid=(bin...  29.7 us
    pallas_call x1, Pallas kernels, gather_strips(): pl.pallas_call(functools.partial(gather_kernel, count), out_shape=jax.Sha...  6.93 us
    unnamed x19, local copies, waits for them, and re-layouts  6.02 us
  transfers between devices with their start and end apart: 2, of which 0 were waited for; matrix products, arithmetic and copies ran while one was open for 4% of the time, Pallas kernels for 3%

commit v1 on v0

v1 whole, which is shorter than its diff:
```python
import functools
import math

import jax
import jax.numpy as jnp
import numpy as np
from jax import lax
from jax.experimental import pallas as pl
from jax.experimental.pallas import tpu as pltpu
from jax.sharding import PartitionSpec as P

NDIR = 36
NFREQ = 32
LEV = 64


HIGHEST = lax.Precision.HIGHEST


def extended(block, sides, width):
    for axis, dim in sides:
        count = lax.axis_size(axis)
        forward = [(i, i + 1) for i in range(count - 1)]
        backward = [(target, source) for source, target in forward]
        low = lax.ppermute(
            lax.slice_in_dim(block, block.shape[dim] - width, None, axis=dim), axis, forward
        )
        high = lax.ppermute(lax.slice_in_dim(block, 0, width, axis=dim), axis, backward)
        block = jnp.concatenate([low, block, high], axis=dim)
    return block


def bin_tables():
    dir_index = jnp.arange(NDIR, dtype=jnp.float32)
    freq_index = jnp.arange(NFREQ, dtype=jnp.float32)
    angles = 2.0 * math.pi * (dir_index + 0.5) / NDIR
    speeds = 0.12 + 0.25 * (NFREQ - 1 - freq_index) / (NFREQ - 1)
    along_x = jnp.repeat(speeds, NDIR) * jnp.tile(jnp.cos(angles), NFREQ)
    along_y = jnp.repeat(speeds, NDIR) * jnp.tile(jnp.sin(angles), NFREQ)
    strength = jnp.repeat(0.06 * (1.0 + freq_index / (NFREQ - 1)), NDIR)
    levels = jnp.arange(LEV, dtype=jnp.float32) + 0.5
    wavenumber = 0.02 * jnp.power(1.15, freq_index)
    decay = jnp.repeat(jnp.exp(-levels[:, None] * wavenumber[None, :]), NDIR, axis=1)
    amplitude = 2.0 / math.sqrt(NDIR * NFREQ)
    cosines = jnp.tile(jnp.cos(angles), NFREQ)
    sines = jnp.tile(jnp.sin(angles), NFREQ)
    drift_table = amplitude * jnp.concatenate(
        [decay * cosines[None, :], decay * sines[None, :]], axis=0
    )
    return (along_x, along_y, strength, drift_table)


def fixed_tables():
    dir_index = np.arange(NDIR, dtype=np.float32)
    freq_index = np.arange(NFREQ, dtype=np.float32)
    angles = 2.0 * math.pi * (dir_index + 0.5) / NDIR
    speeds = 0.12 + 0.25 * (NFREQ - 1 - freq_index) / (NFREQ - 1)
    along_x = np.repeat(speeds, NDIR) * np.tile(np.cos(angles), NFREQ)
    along_y = np.repeat(speeds, NDIR) * np.tile(np.sin(angles), NFREQ)
    strength = np.repeat(0.06 * (1.0 + freq_index / (NFREQ - 1)), NDIR)
    levels = np.arange(LEV, dtype=np.float32) + 0.5
    wavenumber = 0.02 * np.power(np.float32(1.15), freq_index)
    decay = np.repeat(np.exp(-levels[:, None] * wavenumber[None, :]), NDIR, axis=1)
    amplitude = 2.0 / math.sqrt(NDIR * NFREQ)
    cosines = np.tile(np.cos(angles), NFREQ)
    sines = np.tile(np.sin(angles), NFREQ)
    drift_table = amplitude * np.concatenate(
        [decay * cosines[None, :], decay * sines[None, :]], axis=0
    )
    tables = (along_x, along_y, strength, drift_table)
    return tuple(np.asarray(table, dtype=np.float32) for table in tables)


def cell_means(current_cells):
    lon_count = current_cells.shape[0] // 2
    lat_count = current_cells.shape[1] // 2
    return current_cells.reshape(lon_count, 2, lat_count, 2).mean(axis=(1, 3))


def face_fluxes(padded, velocity, dimension):
    face_count = padded.shape[dimension] - 3

    def section(low_edge):
        return lax.slice_in_dim(padded, low_edge, low_edge + face_count, axis=dimension)

    left_value = (-section(0) + 5.0 * section(1) + 2.0 * section(2)) / 6.0
    right_value = (2.0 * section(1) + 5.0 * section(2) - section(3)) / 6.0
    return jnp.maximum(velocity, 0.0) * left_value + jnp.minimum(velocity, 0.0) * right_value


def transport(padded_rows, zonal_flow, along_x, along_y, sea_cells):
    row_count = padded_rows.shape[1] - 4
    spectra = padded_rows[:, 2 : 2 + row_count, :]
    padded_cols = jnp.pad(spectra, ((0, 0), (0, 0), (2, 2)))
    zonal_padded = jnp.pad(zonal_flow, ((0, 0), (1, 1)))
    face_zonal = 0.5 * (zonal_padded[:, :-1] + zonal_padded[:, 1:])
    speed_x = along_x[:, None, None] + face_zonal[None, :, :]
    flux_x = face_fluxes(padded_cols, speed_x, 2)
    flux_y = face_fluxes(padded_rows, along_y[:, None, None], 1)
    change = flux_x[:, :, 1:] - flux_x[:, :, :-1] + flux_y[:, 1:, :] - flux_y[:, :-1, :]
    return sea_cells[None, :, :] * (spectra - change)


def spread_to_ocean(rim, source_map):
    row_count = rim.shape[1] - 2
    col_count = rim.shape[2] - 2
    result = jnp.zeros((rim.shape[0], 2 * col_count, 2 * row_count), jnp.float32)
    for offset in range(9):
        row_shift = offset // 3 - 1
        col_shift = offset % 3 - 1
        shifted = rim[
            :, 1 + row_shift : 1 + row_shift + row_count, 1 + col_shift : 1 + col_shift + col_count
        ]
        shifted = jnp.swapaxes(shifted, 1, 2)
        shifted = jnp.repeat(jnp.repeat(shifted, 2, axis=1), 2, axis=2)
        result = result + jnp.where(source_map[None, :, :] == offset, shifted, jnp.float32(0.0))
    return result


def on_device_plain(spectrum, sea_mask, current, partner_plus, partner_minus, source_map):
    along_x, along_y, strength, drift_table = bin_tables()
    bin_count = NDIR * NFREQ
    local_bins = spectrum.shape[0]
    first_bin = lax.axis_index("bins") * local_bins
    local_x = lax.dynamic_slice_in_dim(along_x, first_bin, local_bins)
    local_y = lax.dynamic_slice_in_dim(along_y, first_bin, local_bins)
    sea_cells = sea_mask.astype(jnp.float32)
    strip_flow = cell_means(current)
    zonal_flow = lax.all_gather(strip_flow, "bins", axis=0, tiled=True).T
    masked = spectrum * sea_cells[None, :, :]
    padded = extended(masked, (("lat", 1),), 2)
    after_first = transport(padded, zonal_flow, local_x, local_y, sea_cells)
    bin_ids = jnp.arange(bin_count, dtype=jnp.int32)
    plus_table = (partner_plus[:, None] == bin_ids[None, :]).astype(jnp.float32)
    minus_table = (partner_minus[:, None] == bin_ids[None, :]).astype(jnp.float32)
    contract_first = (((0,), (0,)), ((), ()))
    arrived = lax.all_to_all(after_first, "bins", split_axis=2, concat_axis=0, tiled=True)
    row_count = arrived.shape[1]
    col_count = arrived.shape[2]
    flat_rows = arrived.reshape(bin_count, row_count * col_count)
    plus_part = jnp.dot(plus_table, flat_rows, precision=HIGHEST)
    minus_part = jnp.dot(minus_table, flat_rows, precision=HIGHEST)
    source = strength[:, None] * (
        flat_rows * flat_rows * (plus_part + minus_part) - 2.0 * flat_rows * plus_part * minus_part
    )
    back = lax.dot_general(plus_table, source, contract_first, precision=HIGHEST) + lax.dot_general(
        minus_table, source, contract_first, precision=HIGHEST
    )
    middle = flat_rows + (source - 0.5 * back)
    drift_rows = jnp.dot(drift_table, middle, precision=HIGHEST)
    middle, drift_rows = (
        middle.reshape(bin_count, row_count, col_count),
        drift_rows.reshape(2 * LEV, row_count, col_count),
    )
    rim = extended(drift_rows, (("bins", 2), ("lat", 1)), 1)
    ocean = spread_to_ocean(rim, source_map)
    stokes = ocean.reshape(2, LEV, ocean.shape[1], ocean.shape[2])
    returned = lax.all_to_all(middle, "bins", split_axis=0, concat_axis=2, tiled=True)
    padded_again = extended(returned, (("lat", 1),), 2)
    second = transport(padded_again, zonal_flow, local_x, local_y, sea_cells)
    return (second, stokes)

MESH = pl.DeviceIdType.MESH
TILE = 128
GROUP = 8
LANES = TILE // GROUP
VMEM = pltpu.VMEM
FORTH = 3
HOME = 6
F32 = jnp.float32


def row_groups(rows):
    edge = rows // 4
    inner = list(range(edge, rows - edge))
    return inner, list(range(edge)) + list(range(rows - edge, rows))


def turn_blocks(tiles):
    lane = lax.broadcasted_iota(jnp.int32, tiles[0].shape, 1) // LANES
    tiles = list(tiles)
    step = 1
    while step < GROUP:
        clear = lax.rem(lane // step, 2) == 0
        for i in range(GROUP):
            if i & step:
                continue
            upper, lower = tiles[i], tiles[i + step]
            tiles[i] = jnp.where(clear, upper, pltpu.roll(lower, step * LANES, 1))
            tiles[i + step] = jnp.where(clear, pltpu.roll(upper, TILE - step * LANES, 1), lower)
        step *= 2
    return tiles


def advect(get, wanted, coefs, face, half, mask):
    cols = face.shape[1]
    lane = lax.broadcasted_iota(jnp.int32, (8, cols), 1)
    at_first = lane == 0
    at_second = lane <= 1
    at_last = lane == cols - 1
    sixth = F32(1.0 / 6.0)
    coef = [jnp.broadcast_to(coefs[:, i : i + 1], (8, cols)) for i in range(6)]
    cache = {}

    def f(row):
        if row not in cache:
            cache[row] = get(row)
        return cache[row]

    results = []
    for row in wanted:
        c = f(row)
        m1 = jnp.where(at_first, 0.0, pltpu.roll(c, 1, 1))
        m2 = jnp.where(at_second, 0.0, pltpu.roll(c, 2, 1))
        p1 = jnp.where(at_last, 0.0, pltpu.roll(c, cols - 1, 1))
        speed = coef[0] + face[row : row + 1, :]
        ahead = speed > 0.0
        part = 3.0 * jnp.where(ahead, m1, c) - jnp.where(ahead, m2, p1)
        flux = (speed * sixth) * (part + 2.0 * (m1 + c))
        end_speed = coef[0] + half[row : row + 1, :]
        end = (end_speed * sixth) * jnp.where(end_speed > 0.0, 5.0 * c - m1, 2.0 * c)
        upper = jnp.where(at_last, end, pltpu.roll(flux, cols - 1, 1))
        along_y = (
            coef[1] * f(row - 2)
            + coef[2] * f(row - 1)
            + coef[3] * c
            + coef[4] * f(row + 1)
            + coef[5] * f(row + 2)
        )
        results.append(mask[row : row + 1, :] * (c - ((upper - flux) + along_y)))
    return results


def halves(value):
    high = value.astype(jnp.bfloat16)
    return high, (value - high.astype(F32)).astype(jnp.bfloat16)


def step_kernel(
    count,
    bands,
    x_ref,
    mask_ref,
    current_ref,
    partner_ref,
    source_ref,
    coef_ref,
    drift_ref,
    out_ref,
    stokes_ref,
    block,
    by_row,
    leaving,
    arrived,
    middle,
    returned,
    plus_table,
    minus_table,
    back_table,
    parts,
    source_parts,
    total,
    mask,
    half,
    face,
    strips,
    low_halo,
    high_halo,
    low_again,
    high_again,
    near,
    chosen_map,
    ocean,
    load_sem,
    strip_send,
    strip_recv,
    halo_send,
    halo_recv,
    in_send,
    in_recv,
    back_send,
    back_recv,
    again_send,
    again_recv,
    near_send,
    near_recv,
    out_sem,
    ocean_sem,
):
    me = lax.axis_index("bins")
    band = lax.axis_index("lat")
    local, rows, cols = block.shape
    bins = local * count
    strip = cols // count
    each = strip // LANES
    pieces = cols // LANES
    chunk_in = local // FORTH
    chunk_out = local // HOME
    tiles = bins // TILE
    width = each * TILE
    across = cols // TILE
    groups = row_groups(rows)
    below = lax.rem(band + bands - 1, bands)
    above = lax.rem(band + 1, bands)
    left = lax.rem(me + count - 1, count)
    right = lax.rem(me + 1, count)
    edges = (jnp.where(band > 0, F32(1.0), F32(0.0)), jnp.where(band < bands - 1, F32(1.0), F32(0.0)))

    def remote(src, dst, send_sem, recv_sem, peer, axis="bins"):
        return pltpu.make_async_remote_copy(
            src_ref=src,
            dst_ref=dst,
            send_sem=send_sem,
            recv_sem=recv_sem,
            device_id={axis: peer},
            device_id_type=MESH,
        )

    def load_copy(part):
        here = pl.ds(part * chunk_in, chunk_in)
        return pltpu.make_async_copy(x_ref.at[here], block.at[here], load_sem.at[part])

    for part in range(FORTH):
        load_copy(part).start()

    barrier = pltpu.get_barrier_semaphore()
    for step in range(1, count):
        pl.semaphore_signal(
            barrier,
            inc=1,
            device_id={"bins": lax.rem(me + step, count)},
            device_id_type=MESH,
        )
    for peer in (below, above):
        pl.semaphore_signal(barrier, inc=1, device_id={"lat": peer}, device_id_type=MESH)

    lons = current_ref.shape[1]
    pairs = current_ref[pl.ds(0, rows, stride=2), :] + current_ref[pl.ds(1, rows, stride=2), :]
    fold = lax.broadcasted_iota(jnp.int32, (lons, TILE), 0) // 2
    fold = jnp.where(fold == lax.broadcasted_iota(jnp.int32, (lons, TILE), 1), F32(0.125), F32(0.0))
    strips[me] = jnp.dot(pairs, fold, precision=HIGHEST, preferred_element_type=F32)
    mask[...] = mask_ref[...].astype(F32)

    pl.semaphore_wait(barrier, count + 1)

    def strip_copy(step):
        peer = lax.rem(me + step, count)
        return remote(strips.at[me], strips.at[me], strip_send.at[step], strip_recv.at[step], peer)

    for step in range(1, count):
        strip_copy(step).start()

    for part in range(FORTH):
        load_copy(part).wait()

        def turn_step(i, carry, part=part):
            here = pl.ds(pl.multiple_of(part * chunk_in + i * 8, 8), 8)
            turned = pltpu.einshape("brl->rbl", block[here, :, :] * mask[...][None])
            for row in range(rows):
                by_row[row, here, :] = turned[row]
            return carry

        lax.fori_loop(0, chunk_in // 8, turn_step, 0)

    halo_copies = [
        remote(
            by_row.at[pl.ds(0, 2)], high_halo, halo_send.at[0], halo_recv.at[0], below, "lat"
        ),
        remote(
            by_row.at[pl.ds(rows - 2, 2)], low_halo, halo_send.at[1], halo_recv.at[1], above, "lat"
        ),
    ]
    for copy in halo_copies:
        copy.start()
    for step in range(1, count):
        strip_copy(step).wait()
    spread = jnp.zeros((rows, cols), F32)
    rest = jnp.zeros((rows, cols - TILE), F32)
    for peer in range(count):
        piece = jnp.concatenate([strips[peer], rest], axis=1)
        spread = spread + (pltpu.roll(piece, peer * strip, 1) if peer else piece)
    half[...] = spread
    first_lane = lax.broadcasted_iota(jnp.int32, (rows, cols), 1) == 0
    face[...] = spread + jnp.where(first_lane, 0.0, pltpu.roll(spread, 1, 1))
    first_bin = me * local

    def fetch(here, low, high):
        def get(row):
            if row < 0:
                return edges[0] * low[row + 2, here, :]
            if row >= rows:
                return edges[1] * high[row - rows, here, :]
            return by_row[row, here, :]

        return get

    def coefs_at(start):
        return coef_ref[pl.ds(pl.multiple_of(first_bin + start, 8), 8), :]

    def in_copy(h, part, step):
        peer = lax.rem(me + step, count)
        src = leaving.at[h, pl.ds(peer * each, each), pl.ds(pl.multiple_of(part * chunk_in, 8), chunk_in), :]
        dst = arrived.at[h, :, pl.ds(pl.multiple_of(first_bin + part * chunk_in, 8), chunk_in), :]
        if step == 0:
            return pltpu.make_async_copy(src, dst, in_recv.at[h, part, 0])
        return remote(src, dst, in_send.at[h, part, step], in_recv.at[h, part, step], peer)

    for h in range(2):
        if h == 1:
            for copy in halo_copies:
                copy.wait()

        def forth_part(part, carry, h=h):
            def forth_step(i, carry):
                start = part * chunk_in + i * 8
                here = pl.ds(pl.multiple_of(start, 8), 8)
                found = advect(
                    fetch(here, low_halo, high_halo),
                    groups[h],
                    coefs_at(start),
                    face[...],
                    half[...],
                    mask[...],
                )
                for t in range(across):
                    turned = turn_blocks([row[:, t * TILE : (t + 1) * TILE] for row in found])
                    for q in range(GROUP):
                        leaving[h, t * GROUP + q, here, :] = turned[q]
                return carry

            lax.fori_loop(0, chunk_in // 8, forth_step, 0)
            for step in range(count):
                in_copy(h, part, step).start()
            return carry

        lax.fori_loop(0, FORTH, forth_part, 0)

    def table_step(tile, carry):
        here = pl.ds(pl.multiple_of(tile * TILE, TILE), TILE)
        along = lax.broadcasted_iota(jnp.int32, (TILE, bins), 1).astype(F32)
        down = (lax.broadcasted_iota(jnp.int32, (TILE, bins), 0) + tile * TILE).astype(F32)
        one = F32(1.0)
        zero = F32(0.0)
        back = jnp.zeros((TILE, bins), F32)
        for which, table in ((0, plus_table), (1, minus_table)):
            column = jnp.broadcast_to(partner_ref[which : which + 1, here], (TILE, TILE)).astype(F32).T
            column = jnp.concatenate([column] * tiles, axis=1)
            table[here, :] = jnp.where(column == along, one, zero).astype(jnp.bfloat16)
            whole = partner_ref[which : which + 1, :].astype(F32)
            back = back + jnp.where(whole == down, one, zero)
        back_table[here, :] = back.astype(jnp.bfloat16)
        return carry

    lax.fori_loop(0, tiles, table_step, 0)

    def back_copy(h, part, step):
        peer = lax.rem(me + step, count)
        src = middle.at[h, :, pl.ds(pl.multiple_of(peer * local + part * chunk_out, 8), chunk_out), :]
        dst = returned.at[h, pl.ds(me * each, each), pl.ds(pl.multiple_of(part * chunk_out, 8), chunk_out), :]
        if step == 0:
            return pltpu.make_async_copy(src, dst, back_recv.at[h, part, 0])
        return remote(src, dst, back_send.at[h, part, step], back_recv.at[h, part, step], peer)

    def pick(table, here, value):
        both = jnp.dot(table[here, :], value[...], preferred_element_type=F32)
        return both[:, :width] + both[:, width:]

    def near_copy(slot):
        if slot == 0:
            src, dst, peer, axis = near.at[pl.ds(1, rows), pl.ds(8, 8)], near.at[pl.ds(1, rows), pl.ds(8 + strip, 8)], left, "bins"
        elif slot == 1:
            src, dst, peer, axis = near.at[pl.ds(1, rows), pl.ds(strip, 8)], near.at[pl.ds(1, rows), pl.ds(0, 8)], right, "bins"
        elif slot == 2:
            src, dst, peer, axis = near.at[1], near.at[rows + 1], below, "lat"
        else:
            src, dst, peer, axis = near.at[rows], near.at[0], above, "lat"
        return remote(src, dst, near_send.at[slot], near_recv.at[slot], peer, axis)

    for h in range(2):

        def await_in(part, carry, h=h):
            for step in range(count):
                in_copy(h, part, step).wait()
            return carry

        lax.fori_loop(0, FORTH, await_in, 0)

        def split_step(tile, carry, h=h):
            here = pl.ds(pl.multiple_of(tile * TILE, TILE), TILE)
            for g in range(each):
                upper, lower = halves(arrived[h, g, here, :])
                parts[here, g * TILE : (g + 1) * TILE] = upper
                parts[here, width + g * TILE : width + (g + 1) * TILE] = lower
            return carry

        lax.fori_loop(0, tiles, split_step, 0)

        def source_step(tile, carry, h=h):
            here = pl.ds(pl.multiple_of(tile * TILE, TILE), TILE)
            plus = pick(plus_table, here, parts)
            minus = pick(minus_table, here, parts)
            strength = coef_ref[here, 6:7]
            for g in range(each):
                lanes = slice(g * TILE, (g + 1) * TILE)
                own = arrived[h, g, here, :]
                p, m = plus[:, lanes], minus[:, lanes]
                source = strength * (own * own * (p + m) - 2.0 * own * p * m)
                upper, lower = halves(source)
                source_parts[here, lanes] = upper
                source_parts[here, width + g * TILE : width + (g + 1) * TILE] = lower
                middle[h, g, here, :] = own + source
            return carry

        lax.fori_loop(0, tiles, source_step, 0)
        total[...] = jnp.zeros_like(total)

        def back_step(tile, carry, h=h):
            here = pl.ds(pl.multiple_of(tile * TILE, TILE), TILE)
            back = pick(back_table, here, source_parts)
            done = []
            for g in range(each):
                value = middle[h, g, here, :] - 0.5 * back[:, g * TILE : (g + 1) * TILE]
                middle[h, g, here, :] = value
                done.append(value)
            total[...] += jnp.dot(
                drift_ref[:, here],
                jnp.concatenate(done, axis=1),
                precision=HIGHEST,
                preferred_element_type=F32,
            )
            return carry

        lax.fori_loop(0, tiles, back_step, 0)
        for g in range(each):
            points = total[:, g * TILE : (g + 1) * TILE].T
            for at, row in enumerate(groups[h]):
                near[1 + row, 8 + g * LANES : 8 + (g + 1) * LANES, :] = points[at * LANES : (at + 1) * LANES, :]
        if h == 1:
            near_copy(0).start()
            near_copy(1).start()

        def send_back(part, carry, h=h):
            for step in range(count):
                back_copy(h, part, step).start()
            return carry

        lax.fori_loop(0, HOME, send_back, 0)

    near_copy(0).wait()
    near_copy(1).wait()
    side = (jnp.where(me > 0, F32(1.0), F32(0.0)), jnp.where(me < count - 1, F32(1.0), F32(0.0)))
    inner = pl.ds(1, rows)
    near[inner, 0:8, :] = near[inner, 0:8, :] * side[0]
    near[inner, 8 + strip : 16 + strip, :] = near[inner, 8 + strip : 16 + strip, :] * side[1]
    near_copy(2).start()
    near_copy(3).start()

    chosen_map[...] = jnp.zeros_like(chosen_map)
    sources = source_ref[...]
    third = jnp.where(sources >= 3, 1, 0) + jnp.where(sources >= 6, 1, 0)
    extent = strip + 16
    columns = lax.broadcasted_iota(jnp.int32, sources.shape, 1) // 2
    chosen_map[:, :lons] = third * extent + 7 + columns + (sources - 3 * third)
    near_copy(2).wait()
    near_copy(3).wait()
    near[0] = near[0] * edges[0]
    near[rows + 1] = near[rows + 1] * edges[1]

    depth = 3 * extent
    profiles = near.shape[2]
    ocean_copies = []
    for octet in range(2 * rows // 8):
        found = []
        for row in range(octet * 4, octet * 4 + 4):
            window = near[row : row + 3].reshape(depth, profiles)
            down = lax.broadcasted_iota(jnp.int32, (depth, TILE), 0)
            chosen = [
                jnp.where(down == chosen_map[lat : lat + 1, :], F32(1.0), F32(0.0))
                for lat in (2 * row, 2 * row + 1)
            ]
            both = lax.dot_general(
                window,
                jnp.concatenate(chosen, axis=1),
                (((0,), (0,)), ((), ())),
                precision=HIGHEST,
                preferred_element_type=F32,
            )
            found += [both[:, :TILE], both[:, TILE:]]
        here = pl.ds(octet * 8, 8)
        ocean[:, here, :] = pltpu.einshape("ypl->pyl", jnp.stack(found))[:, :, :lons]
        copy = pltpu.make_async_copy(ocean.at[:, here, :], stokes_ref.at[:, here, :], ocean_sem.at[octet])
        copy.start()
        ocean_copies.append(copy)

    def again_copy(part, slot):
        here = pl.ds(pl.multiple_of(part * chunk_out, 8), chunk_out)
        if slot == 0:
            src, dst, peer = by_row.at[pl.ds(0, 2), here, :], high_again.at[:, here, :], below
        else:
            src, dst, peer = by_row.at[pl.ds(rows - 2, 2), here, :], low_again.at[:, here, :], above
        return remote(src, dst, again_send.at[slot, part], again_recv.at[slot, part], peer, "lat")

    def out_copy(part):
        here = pl.ds(part * chunk_out, chunk_out)
        return pltpu.make_async_copy(block.at[here], out_ref.at[here], out_sem.at[part])

    def home_part(turn, carry):
        @pl.when(turn < HOME)
        def _():
            for h in range(2):
                for step in range(count):
                    back_copy(h, turn, step).wait()

            def unpack_step(i, carry):
                here = pl.ds(pl.multiple_of(turn * chunk_out + i * 8, 8), 8)
                for h in range(2):
                    for t in range(across):
                        turned = turn_blocks([returned[h, t * GROUP + q, here, :] for q in range(GROUP)])
                        for at, row in enumerate(groups[h]):
                            by_row[row, here, t * TILE : (t + 1) * TILE] = turned[at]
                return carry

            lax.fori_loop(0, chunk_out // 8, unpack_step, 0)
            again_copy(turn, 0).start()
            again_copy(turn, 1).start()

        @pl.when(turn > 0)
        def _():
            part = turn - 1
            again_copy(part, 0).wait()
            again_copy(part, 1).wait()

            def home_step(i, carry):
                start = part * chunk_out + i * 8
                here = pl.ds(pl.multiple_of(start, 8), 8)
                found = advect(
                    fetch(here, low_again, high_again),
                    list(range(rows)),
                    coefs_at(start),
                    face[...],
                    half[...],
                    mask[...],
                )
                block[here, :, :] = pltpu.einshape("rbl->brl", jnp.stack(found))
                return carry

            lax.fori_loop(0, chunk_out // 8, home_step, 0)
            out_copy(part).start()

        return carry

    lax.fori_loop(0, HOME + 1, home_part, 0)
    for part in range(HOME):
        out_copy(part).wait()
    for copy in ocean_copies:
        copy.wait()


def step_call(spectrum, sea_mask, current, partners, source_map, coefs, drift_table, count, bands):
    local, rows, cols = spectrum.shape
    bins = local * count
    profiles = drift_table.shape[0]
    lats, lons = source_map.shape
    strip = cols // count
    each = strip // LANES
    pieces = cols // LANES
    vmem = pl.BlockSpec(memory_space=VMEM)
    hbm = pl.BlockSpec(memory_space=pl.ANY)
    dma = pltpu.SemaphoreType.DMA
    return pl.pallas_call(
        functools.partial(step_kernel, count, bands),
        out_shape=(
            jax.ShapeDtypeStruct(spectrum.shape, F32),
            jax.ShapeDtypeStruct((profiles, lats, lons), F32),
        ),
        in_specs=[hbm] + [vmem] * 6,
        out_specs=(hbm, hbm),
        scratch_shapes=[
            VMEM((local, rows, cols), F32),
            VMEM((rows, local, cols), F32),
            VMEM((2, pieces, local, TILE), F32),
            VMEM((2, each, bins, TILE), F32),
            VMEM((2, each, bins, TILE), F32),
            VMEM((2, pieces, local, TILE), F32),
            VMEM((bins, bins), jnp.bfloat16),
            VMEM((bins, bins), jnp.bfloat16),
            VMEM((bins, bins), jnp.bfloat16),
            VMEM((bins, 2 * each * TILE), jnp.bfloat16),
            VMEM((bins, 2 * each * TILE), jnp.bfloat16),
            VMEM((profiles, each * TILE), F32),
            VMEM((rows, cols), F32),
            VMEM((rows, cols), F32),
            VMEM((rows, cols), F32),
            VMEM((count, rows, TILE), F32),
            VMEM((2, local, cols), F32),
            VMEM((2, local, cols), F32),
            VMEM((2, local, cols), F32),
            VMEM((2, local, cols), F32),
            VMEM((rows + 2, strip + 16, profiles), F32),
            VMEM((lats, TILE), jnp.int32),
            VMEM((profiles, lats, lons), F32),
            dma((FORTH,)),
            dma((count,)),
            dma((count,)),
            dma((2,)),
            dma((2,)),
            dma((2, FORTH, count)),
            dma((2, FORTH, count)),
            dma((2, HOME, count)),
            dma((2, HOME, count)),
            dma((2, HOME)),
            dma((2, HOME)),
            dma((4,)),
            dma((4,)),
            dma((HOME,)),
            dma((lats // 8,)),
        ],
        compiler_params=pltpu.CompilerParams(
            collective_id=0, has_side_effects=True, vmem_limit_bytes=60 * 1024 * 1024
        ),
    )(spectrum, sea_mask, current, partners, source_map, coefs, drift_table)


def on_device_fast(spectrum, sea_mask, current, partner_plus, partner_minus, source_map):
    count = lax.axis_size("bins")
    bands = lax.axis_size("lat")
    along_x, along_y, strength, drift_table = fixed_tables()
    forth = np.maximum(along_y, 0.0) / 6.0
    back = np.minimum(along_y, 0.0) / 6.0
    coefs = np.stack(
        [
            along_x,
            forth,
            -6.0 * forth - 2.0 * back,
            3.0 * forth - 3.0 * back,
            2.0 * forth + 6.0 * back,
            -back,
            strength,
            np.zeros_like(forth),
        ],
        axis=1,
    ).astype(np.float32)
    second, stokes = step_call(
        spectrum,
        sea_mask,
        current.T,
        jnp.stack([partner_plus, partner_minus]),
        source_map.T,
        jnp.asarray(coefs),
        jnp.asarray(drift_table),
        count,
        bands,
    )
    lons, lats = source_map.shape
    return (second, jnp.swapaxes(stokes.reshape(2, LEV, lats, lons), 2, 3))


def on_device(spectrum, sea_mask, current, partner_plus, partner_minus, source_map):
    count = lax.axis_size("bins")
    bins, rows, cols = spectrum.shape
    bands = lax.axis_size("lat")
    lons, lats = source_map.shape
    strip = cols // count
    fits = (
        rows == 2 * GROUP
        and bins % (8 * FORTH) == 0
        and bins % (8 * HOME) == 0
        and cols % TILE == 0
        and strip * count == cols
        and strip % LANES == 0
        and strip <= TILE
        and bins * count % TILE == 0
        and lats == 2 * rows
        and lons == 2 * strip
        and lons <= TILE
        and count > 2
        and bands > 2
    )
    body = on_device_fast if fits else on_device_plain
    return body(spectrum, sea_mask, current, partner_plus, partner_minus, source_map)


def solution(mesh):
    return jax.shard_map(
        on_device,
        mesh=mesh,
        in_specs=(
            P("bins", "lat", None),
            P("lat", None),
            P("bins", "lat"),
            P(),
            P(),
            P("bins", "lat"),
        ),
        out_specs=(P("bins", "lat", None), P(None, None, "bins", "lat")),
        check_vma=False,
    )
```

time: 240 us -> 188 us (0.78)
  Pallas kernels: 212 us -> 178 us
  local copies, waits for them, and re-layouts: 17.7 us -> 6.89 us
  starting transfers between devices: 5.63 us -> 0 us
    pallas_call x4 -> x1, Pallas kernels: 212 us -> 178 us  [step_call(): pl.pallas_call(functools.partial(step_kernel, count, bands), out_shape=(j...]
    ppermute x2 -> x0, starting transfers between devices: 5.63 us -> none  [the longest x1 3.71 us: exchange_rows(): lax.ppermute(high_side, 'lat', forward)]
    broadcast_in_dim x6 -> x0, local copies, waits for them, and re-layouts: 4.57 us -> none  [the longest x1 1.03 us: middle_call(): partner_plus[:, None]]
    unnamed x19 -> x4, local copies, waits for them, and re-layouts: 6.02 us -> 5.49 us
  transfers between devices with their start and end apart: 2 -> 0, of which waited for: 0 -> 0; matrix products, arithmetic and copies ran while one was open for 4% -> 0% of each run, Pallas kernels for 3% -> 0%
where the time goes in v1:
time: 188 us; the launch traced here: 186 us
  Pallas kernels  178 us (95%)
  local copies, waits for them, and re-layouts  6.89 us (4%)
    pallas_call x1, Pallas kernels, step_call(): pl.pallas_call(functools.partial(step_kernel, count, bands), out_shape=(j...  178 us
    unnamed x4, local copies, waits for them, and re-layouts  5.49 us

profile of v1, /device:TPU:9, one launch (start us, length us, event | category | flops | bytes accessed | tf_op | source)
XLA Modules:
  0.0 186.0 jit_solution(8437501581571716477)
XLA Ops:
  0.6 0.7 stack.9
  1.3 0.7 stack.10
  2.0 0.6 pad_add_fusion.partner_ref
  2.6 177.8 %shard_map.95 = (f32[144,16,384]{2,1,0:T(8,128)}, f32[128,32,96]{2,1,0:T(8,128)}) custom-call(f32[144,16,384]{2,1,0:T(8,128)} %x_ref.1, s32[16,384]{1,0:T(8,128)} %mask_ref.1, f32[32,96]{1,0:T(8,128)} %bitcast.6, s32[2,1152]{1,0:T(2,128)} %pad_add_fusion.partner_ref, s32[32,96]{1,0:T(8,128)} %bitcast.7, f32[1152,8]{1,0:T(8,128)} %constant.4.clone.coef_ref, ...), custom_call_target="tpu_custom_call" | custom-call | tf_op jit(solution)/shard_map/pallas_call | solution.py:670
  180.5 0.0 copy-start
  180.5 4.2 %copy.12 = f32[144,16,384]{2,1,0:T(8,128)} copy(f32[144,16,384]{2,1,0:T(8,128)} %get-tuple-element.8) | data formatting | bytes 7077888
  184.6 0.0 copy-done
  184.7 1.3 copy.13
Async XLA Ops:
  180.5 4.2 %copy-start = (f32[128,32,96]{2,1,0:T(8,128)S(1)}, f32[128,32,96]{2,1,0:T(8,128)}, u32[]{:S(2)}) copy-start(f32[128,32,96]{2,1,0:T(8,128)} %get-tuple-element.5) | copy-start | bytes 4718596

commit v2 on v1

--- a/solution.py
+++ b/solution.py
@@ -165,8 +165,13 @@
 GROUP = 8
 LANES = TILE // GROUP
 VMEM = pltpu.VMEM
-FORTH = 3
-HOME = 6
+LOADS = 3
+STEPS = 9
+LEAD = 2
+FORTH = ((0, 1, 5, 9), (0, 4, 9))
+HOME = ((0, 3, 6, 8, 9), (0, 3, 6, 9))
+QUEUE = ((0, 0), (0, 1), (1, 0), (1, 1), (1, 2), (0, 2), (0, 3))
+AHEAD = 2
 F32 = jnp.float32
 
 
@@ -240,12 +245,13 @@
     count,
     bands,
     x_ref,
-    mask_ref,
-    current_ref,
-    partner_ref,
-    source_ref,
-    coef_ref,
-    drift_ref,
+    mask_hbm,
+    current_hbm,
+    plus_hbm,
+    minus_hbm,
+    source_hbm,
+    table_hbm,
+    drift_hbm,
     out_ref,
     stokes_ref,
     block,
@@ -269,9 +275,19 @@
     low_again,
     high_again,
     near,
+    columns,
     chosen_map,
     ocean,
+    coefs,
+    table,
+    drift_ref,
+    mask_ref,
+    current_ref,
+    plus_ref,
+    minus_ref,
+    source_ref,
     load_sem,
+    table_sem,
     strip_send,
     strip_recv,
     halo_send,
@@ -294,8 +310,7 @@
     strip = cols // count
     each = strip // LANES
     pieces = cols // LANES
-    chunk_in = local // FORTH
-    chunk_out = local // HOME
+    unit = local // STEPS
     tiles = bins // TILE
     width = each * TILE
     across = cols // TILE
@@ -316,13 +331,35 @@
             device_id_type=MESH,
         )
 
+    chunk_load = local // LOADS
+
     def load_copy(part):
-        here = pl.ds(part * chunk_in, chunk_in)
+        here = pl.ds(part * chunk_load, chunk_load)
         return pltpu.make_async_copy(x_ref.at[here], block.at[here], load_sem.at[part])
 
-    for part in range(FORTH):
+    first_bin = me * local
+    own_bins = pl.ds(pl.multiple_of(first_bin, 8), local)
+    table_copies = [
+        pltpu.make_async_copy(src, dst, table_sem.at[i])
+        for i, (src, dst) in enumerate(
+            (
+                (current_hbm, current_ref),
+                (mask_hbm, mask_ref),
+                (table_hbm.at[own_bins], coefs),
+                (table_hbm, table),
+                (drift_hbm, drift_ref),
+                (plus_hbm, plus_ref),
+                (minus_hbm, minus_ref),
+                (source_hbm, source_ref),
+            )
+        )
+    ]
+    for copy in table_copies[:2]:
+        copy.start()
+    for part in range(LOADS):
         load_copy(part).start()
 
+    near[...] = jnp.zeros_like(near)
     barrier = pltpu.get_barrier_semaphore()
     for step in range(1, count):
         pl.semaphore_signal(
@@ -335,6 +372,8 @@
         pl.semaphore_signal(barrier, inc=1, device_id={"lat": peer}, device_id_type=MESH)
 
     lons = current_ref.shape[1]
+    for copy in table_copies[:2]:
+        copy.wait()
     pairs = current_ref[pl.ds(0, rows, stride=2), :] + current_ref[pl.ds(1, rows, stride=2), :]
     fold = lax.broadcasted_iota(jnp.int32, (lons, TILE), 0) // 2
     fold = jnp.where(fold == lax.broadcasted_iota(jnp.int32, (lons, TILE), 1), F32(0.125), F32(0.0))
@@ -350,17 +389,17 @@
     for step in range(1, count):
         strip_copy(step).start()
 
-    for part in range(FORTH):
+    for part in range(LOADS):
         load_copy(part).wait()
 
         def turn_step(i, carry, part=part):
-            here = pl.ds(pl.multiple_of(part * chunk_in + i * 8, 8), 8)
+            here = pl.ds(pl.multiple_of(part * chunk_load + i * 8, 8), 8)
             turned = pltpu.einshape("brl->rbl", block[here, :, :] * mask[...][None])
             for row in range(rows):
                 by_row[row, here, :] = turned[row]
             return carry
 
-        lax.fori_loop(0, chunk_in // 8, turn_step, 0)
+        lax.fori_loop(0, chunk_load // 8, turn_step, 0)
 
     halo_copies = [
         remote(
@@ -370,8 +409,9 @@
             by_row.at[pl.ds(rows - 2, 2)], low_halo, halo_send.at[1], halo_recv.at[1], above, "lat"
         ),
     ]
-    for copy in halo_copies:
+    for copy in halo_copies + table_copies[2:]:
         copy.start()
+    table_copies[2].wait()
     for step in range(1, count):
         strip_copy(step).wait()
     spread = jnp.zeros((rows, cols), F32)
@@ -382,7 +422,6 @@
     half[...] = spread
     first_lane = lax.broadcasted_iota(jnp.int32, (rows, cols), 1) == 0
     face[...] = spread + jnp.where(first_lane, 0.0, pltpu.roll(spread, 1, 1))
-    first_bin = me * local
 
     def fetch(here, low, high):
         def get(row):
@@ -395,12 +434,16 @@
         return get
 
     def coefs_at(start):
-        return coef_ref[pl.ds(pl.multiple_of(first_bin + start, 8), 8), :]
+        return coefs[pl.ds(pl.multiple_of(start, 8), 8), :]
+
+    def reach(cuts, part):
+        return cuts[part] * unit, (cuts[part + 1] - cuts[part]) * unit
 
     def in_copy(h, part, step):
         peer = lax.rem(me + step, count)
-        src = leaving.at[h, pl.ds(peer * each, each), pl.ds(pl.multiple_of(part * chunk_in, 8), chunk_in), :]
-        dst = arrived.at[h, :, pl.ds(pl.multiple_of(first_bin + part * chunk_in, 8), chunk_in), :]
+        at, size = reach(FORTH[h], part)
+        src = leaving.at[h, pl.ds(peer * each, each), pl.ds(at, size), :]
+        dst = arrived.at[h, :, pl.ds(pl.multiple_of(first_bin + at, 8), size), :]
         if step == 0:
             return pltpu.make_async_copy(src, dst, in_recv.at[h, part, 0])
         return remote(src, dst, in_send.at[h, part, step], in_recv.at[h, part, step], peer)
@@ -410,9 +453,9 @@
             for copy in halo_copies:
                 copy.wait()
 
-        def forth_part(part, carry, h=h):
+        def forth_turn(turn, carry, h=h):
             def forth_step(i, carry):
-                start = part * chunk_in + i * 8
+                start = turn * unit + i * 8
                 here = pl.ds(pl.multiple_of(start, 8), 8)
                 found = advect(
                     fetch(here, low_halo, high_halo),
@@ -428,12 +471,17 @@
                         leaving[h, t * GROUP + q, here, :] = turned[q]
                 return carry
 
-            lax.fori_loop(0, chunk_in // 8, forth_step, 0)
-            for step in range(count):
-                in_copy(h, part, step).start()
+            lax.fori_loop(0, unit // 8, forth_step, 0)
+            for part, end in enumerate(FORTH[h][1:]):
+
+                @pl.when(turn == end - 1)
+                def _(part=part):
+                    for step in range(1, count + 1):
+                        in_copy(h, part, step % count).start()
+
             return carry
 
-        lax.fori_loop(0, FORTH, forth_part, 0)
+        lax.fori_loop(0, STEPS, forth_turn, 0)
 
     def table_step(tile, carry):
         here = pl.ds(pl.multiple_of(tile * TILE, TILE), TILE)
@@ -442,34 +490,47 @@
         one = F32(1.0)
         zero = F32(0.0)
         back = jnp.zeros((TILE, bins), F32)
-        for which, table in ((0, plus_table), (1, minus_table)):
-            column = jnp.broadcast_to(partner_ref[which : which + 1, here], (TILE, TILE)).astype(F32).T
+        for partner_ref, picks in ((plus_ref, plus_table), (minus_ref, minus_table)):
+            column = jnp.broadcast_to(partner_ref[here][None, :], (TILE, TILE)).astype(F32).T
             column = jnp.concatenate([column] * tiles, axis=1)
-            table[here, :] = jnp.where(column == along, one, zero).astype(jnp.bfloat16)
-            whole = partner_ref[which : which + 1, :].astype(F32)
+            picks[here, :] = jnp.where(column == along, one, zero).astype(jnp.bfloat16)
+            whole = partner_ref[...][None, :].astype(F32)
             back = back + jnp.where(whole == down, one, zero)
         back_table[here, :] = back.astype(jnp.bfloat16)
         return carry
 
+    for copy in table_copies[3:]:
+        copy.wait()
     lax.fori_loop(0, tiles, table_step, 0)
 
     def back_copy(h, part, step):
         peer = lax.rem(me + step, count)
-        src = middle.at[h, :, pl.ds(pl.multiple_of(peer * local + part * chunk_out, 8), chunk_out), :]
-        dst = returned.at[h, pl.ds(me * each, each), pl.ds(pl.multiple_of(part * chunk_out, 8), chunk_out), :]
+        at, size = reach(HOME[h], part)
+        src = middle.at[h, :, pl.ds(pl.multiple_of(peer * local + at, 8), size), :]
+        dst = returned.at[h, pl.ds(me * each, each), pl.ds(at, size), :]
         if step == 0:
             return pltpu.make_async_copy(src, dst, back_recv.at[h, part, 0])
         return remote(src, dst, back_send.at[h, part, step], back_recv.at[h, part, step], peer)
 
+    def send_back(at):
+        for step in range(1, count + 1):
+            back_copy(*QUEUE[at], step % count).start()
+
+    def await_back(at):
+        for step in range(count):
+            back_copy(*QUEUE[at], step).wait()
+        if at + AHEAD < len(QUEUE):
+            send_back(at + AHEAD)
+
     def pick(table, here, value):
         both = jnp.dot(table[here, :], value[...], preferred_element_type=F32)
         return both[:, :width] + both[:, width:]
 
     def near_copy(slot):
         if slot == 0:
-            src, dst, peer, axis = near.at[pl.ds(1, rows), pl.ds(8, 8)], near.at[pl.ds(1, rows), pl.ds(8 + strip, 8)], left, "bins"
+            src, dst, peer, axis = columns.at[0], columns.at[2], left, "bins"
         elif slot == 1:
-            src, dst, peer, axis = near.at[pl.ds(1, rows), pl.ds(strip, 8)], near.at[pl.ds(1, rows), pl.ds(0, 8)], right, "bins"
+            src, dst, peer, axis = columns.at[1], columns.at[3], right, "bins"
         elif slot == 2:
             src, dst, peer, axis = near.at[1], near.at[rows + 1], below, "lat"
         else:
@@ -477,13 +538,9 @@
         return remote(src, dst, near_send.at[slot], near_recv.at[slot], peer, axis)
 
     for h in range(2):
-
-        def await_in(part, carry, h=h):
+        for part in range(len(FORTH[h]) - 1):
             for step in range(count):
                 in_copy(h, part, step).wait()
-            return carry
-
-        lax.fori_loop(0, FORTH, await_in, 0)
 
         def split_step(tile, carry, h=h):
             here = pl.ds(pl.multiple_of(tile * TILE, TILE), TILE)
@@ -499,7 +556,7 @@
             here = pl.ds(pl.multiple_of(tile * TILE, TILE), TILE)
             plus = pick(plus_table, here, parts)
             minus = pick(minus_table, here, parts)
-            strength = coef_ref[here, 6:7]
+            strength = table[here, 6:7]
             for g in range(each):
                 lanes = slice(g * TILE, (g + 1) * TILE)
                 own = arrived[h, g, here, :]
@@ -536,22 +593,23 @@
             for at, row in enumerate(groups[h]):
                 near[1 + row, 8 + g * LANES : 8 + (g + 1) * LANES, :] = points[at * LANES : (at + 1) * LANES, :]
         if h == 1:
+            for row in range(rows):
+                columns[0, row : row + 1, :] = near[1 + row, 8:9, :]
+                columns[1, row : row + 1, :] = near[1 + row, 7 + strip : 8 + strip, :]
             near_copy(0).start()
             near_copy(1).start()
 
-        def send_back(part, carry, h=h):
-            for step in range(count):
-                back_copy(h, part, step).start()
-            return carry
-
-        lax.fori_loop(0, HOME, send_back, 0)
-
+        for at, (which, part) in enumerate(QUEUE[:AHEAD]):
+            if which == h:
+                send_back(at)
+
+    await_back(0)
     near_copy(0).wait()
     near_copy(1).wait()
     side = (jnp.where(me > 0, F32(1.0), F32(0.0)), jnp.where(me < count - 1, F32(1.0), F32(0.0)))
-    inner = pl.ds(1, rows)
-    near[inner, 0:8, :] = near[inner, 0:8, :] * side[0]
-    near[inner, 8 + strip : 16 + strip, :] = near[inner, 8 + strip : 16 + strip, :] * side[1]
+    for row in range(rows):
+        near[1 + row, 7:8, :] = columns[3, row : row + 1, :] * side[0]
+        near[1 + row, 8 + strip : 9 + strip, :] = columns[2, row : row + 1, :] * side[1]
     near_copy(2).start()
     near_copy(3).start()
 
@@ -559,8 +617,8 @@
     sources = source_ref[...]
     third = jnp.where(sources >= 3, 1, 0) + jnp.where(sources >= 6, 1, 0)
     extent = strip + 16
-    columns = lax.broadcasted_iota(jnp.int32, sources.shape, 1) // 2
-    chosen_map[:, :lons] = third * extent + 7 + columns + (sources - 3 * third)
+    column = lax.broadcasted_iota(jnp.int32, sources.shape, 1) // 2
+    chosen_map[:, :lons] = third * extent + 7 + column + (sources - 3 * third)
     near_copy(2).wait()
     near_copy(3).wait()
     near[0] = near[0] * edges[0]
@@ -593,7 +651,7 @@
         ocean_copies.append(copy)
 
     def again_copy(part, slot):
-        here = pl.ds(pl.multiple_of(part * chunk_out, 8), chunk_out)
+        here = pl.ds(pl.multiple_of(part * unit, 8), unit)
         if slot == 0:
             src, dst, peer = by_row.at[pl.ds(0, 2), here, :], high_again.at[:, here, :], below
         else:
@@ -601,37 +659,43 @@
         return remote(src, dst, again_send.at[slot, part], again_recv.at[slot, part], peer, "lat")
 
     def out_copy(part):
-        here = pl.ds(part * chunk_out, chunk_out)
+        here = pl.ds(part * unit, unit)
         return pltpu.make_async_copy(block.at[here], out_ref.at[here], out_sem.at[part])
 
+    def unpack(h, turn):
+        for at, (which, part) in enumerate(QUEUE):
+            if which == h and at > 1:
+
+                @pl.when(turn == HOME[h][part])
+                def _(at=at):
+                    await_back(at)
+
+        def unpack_step(i, carry):
+            here = pl.ds(pl.multiple_of(turn * unit + i * 8, 8), 8)
+            for t in range(across):
+                turned = turn_blocks([returned[h, t * GROUP + q, here, :] for q in range(GROUP)])
+                for at, row in enumerate(groups[h]):
+                    by_row[row, here, t * TILE : (t + 1) * TILE] = turned[at]
+            return carry
+
+        lax.fori_loop(0, unit // 8, unpack_step, 0)
+
     def home_part(turn, carry):
-        @pl.when(turn < HOME)
+        @pl.when(turn < STEPS)
         def _():
-            for h in range(2):
-                for step in range(count):
-                    back_copy(h, turn, step).wait()
-
-            def unpack_step(i, carry):
-                here = pl.ds(pl.multiple_of(turn * chunk_out + i * 8, 8), 8)
-                for h in range(2):
-                    for t in range(across):
-                        turned = turn_blocks([returned[h, t * GROUP + q, here, :] for q in range(GROUP)])
-                        for at, row in enumerate(groups[h]):
-                            by_row[row, here, t * TILE : (t + 1) * TILE] = turned[at]
-                return carry
-
-            lax.fori_loop(0, chunk_out // 8, unpack_step, 0)
+            unpack(1, turn)
             again_copy(turn, 0).start()
             again_copy(turn, 1).start()
 
-        @pl.when(turn > 0)
+        @pl.when(turn >= LEAD)
         def _():
-            part = turn - 1
+            part = turn - LEAD
+            unpack(0, part)
             again_copy(part, 0).wait()
             again_copy(part, 1).wait()
 
             def home_step(i, carry):
-                start = part * chunk_out + i * 8
+                start = part * unit + i * 8
                 here = pl.ds(pl.multiple_of(start, 8), 8)
                 found = advect(
                     fetch(here, low_again, high_again),
@@ -644,19 +708,20 @@
                 block[here, :, :] = pltpu.einshape("rbl->brl", jnp.stack(found))
                 return carry
 
-            lax.fori_loop(0, chunk_out // 8, home_step, 0)
+            lax.fori_loop(0, unit // 8, home_step, 0)
             out_copy(part).start()
 
         return carry
 
-    lax.fori_loop(0, HOME + 1, home_part, 0)
-    for part in range(HOME):
+    await_back(1)
+    lax.fori_loop(0, STEPS + LEAD, home_part, 0)
+    for part in range(STEPS):
         out_copy(part).wait()
     for copy in ocean_copies:
         copy.wait()
 
 
-def step_call(spectrum, sea_mask, current, partners, source_map, coefs, drift_table, count, bands):
+def step_call(spectrum, sea_mask, current, plus, minus, source_map, coefs, drift_table, count, bands):
     local, rows, cols = spectrum.shape
     bins = local * count
     profiles = drift_table.shape[0]
@@ -664,16 +729,17 @@
     strip = cols // count
     each = strip // LANES
     pieces = cols // LANES
-    vmem = pl.BlockSpec(memory_space=VMEM)
     hbm = pl.BlockSpec(memory_space=pl.ANY)
     dma = pltpu.SemaphoreType.DMA
+    forth = max(len(cuts) for cuts in FORTH) - 1
+    home = max(len(cuts) for cuts in HOME) - 1
     return pl.pallas_call(
         functools.partial(step_kernel, count, bands),
         out_shape=(
             jax.ShapeDtypeStruct(spectrum.shape, F32),
             jax.ShapeDtypeStruct((profiles, lats, lons), F32),
         ),
-        in_specs=[hbm] + [vmem] * 6,
+        in_specs=[pl.BlockSpec(memory_space=pltpu.HBM)] * 8,
         out_specs=(hbm, hbm),
         scratch_shapes=[
             VMEM((local, rows, cols), F32),
@@ -697,28 +763,38 @@
             VMEM((2, local, cols), F32),
             VMEM((2, local, cols), F32),
             VMEM((rows + 2, strip + 16, profiles), F32),
+            VMEM((4, rows, profiles), F32),
             VMEM((lats, TILE), jnp.int32),
             VMEM((profiles, lats, lons), F32),
-            dma((FORTH,)),
+            VMEM((local, coefs.shape[1]), F32),
+            VMEM(coefs.shape, F32),
+            VMEM(drift_table.shape, F32),
+            VMEM(sea_mask.shape, jnp.int32),
+            VMEM(current.shape, F32),
+            VMEM(plus.shape, jnp.int32),
+            VMEM(minus.shape, jnp.int32),
+            VMEM(source_map.shape, jnp.int32),
+            dma((LOADS,)),
+            dma((8,)),
             dma((count,)),
             dma((count,)),
             dma((2,)),
             dma((2,)),
-            dma((2, FORTH, count)),
-            dma((2, FORTH, count)),
-            dma((2, HOME, count)),
-            dma((2, HOME, count)),
-            dma((2, HOME)),
-            dma((2, HOME)),
+            dma((2, forth, count)),
+            dma((2, forth, count)),
+            dma((2, home, count)),
+            dma((2, home, count)),
+            dma((2, STEPS)),
+            dma((2, STEPS)),
             dma((4,)),
             dma((4,)),
-            dma((HOME,)),
+            dma((STEPS,)),
             dma((lats // 8,)),
         ],
         compiler_params=pltpu.CompilerParams(
-            collective_id=0, has_side_effects=True, vmem_limit_bytes=60 * 1024 * 1024
+            collective_id=0, has_side_effects=True, vmem_limit_bytes=58 * 1024 * 1024
         ),
-    )(spectrum, sea_mask, current, partners, source_map, coefs, drift_table)
+    )(spectrum, sea_mask, current, plus, minus, source_map, coefs, drift_table)
 
 
 def on_device_fast(spectrum, sea_mask, current, partner_plus, partner_minus, source_map):
@@ -744,7 +820,8 @@
         spectrum,
         sea_mask,
         current.T,
-        jnp.stack([partner_plus, partner_minus]),
+        partner_plus,
+        partner_minus,
         source_map.T,
         jnp.asarray(coefs),
         jnp.asarray(drift_table),
@@ -763,8 +840,8 @@
     strip = cols // count
     fits = (
         rows == 2 * GROUP
-        and bins % (8 * FORTH) == 0
-        and bins % (8 * HOME) == 0
+        and bins % (8 * STEPS) == 0
+        and bins % (8 * LOADS) == 0
         and cols % TILE == 0
         and strip * count == cols
         and strip % LANES == 0

time: 188 us -> 178 us (0.947)
  Pallas kernels: 178 us -> 170 us
    pallas_call x1, Pallas kernels: 178 us -> 170 us  [step_call(): pl.pallas_call(functools.partial(step_kernel, count, bands), out_shape=(j...]
where the time goes in v2:
time: 178 us; the launch traced here: 176 us
  Pallas kernels  170 us (96%)
  local copies, waits for them, and re-layouts  5.49 us (3%)
    pallas_call x1, Pallas kernels, step_call(): pl.pallas_call(functools.partial(step_kernel, count, bands), out_shape=(j...  170 us
    unnamed x4, local copies, waits for them, and re-layouts  5.49 us

profile of v2, /device:TPU:9, one launch (start us, length us, event | category | flops | bytes accessed | tf_op | source)
XLA Modules:
  0.0 175.9 jit_solution(10054489329786208145)
XLA Ops:
  0.6 169.7 %shard_map.95 = (f32[144,16,384]{2,1,0:T(8,128)}, f32[128,32,96]{2,1,0:T(8,128)}) custom-call(f32[144,16,384]{2,1,0:T(8,128)} %x_ref.1, s32[16,384]{1,0:T(8,128)} %mask_hbm.1, f32[32,96]{1,0:T(8,128)} %bitcast.6, s32[1152]{0:T(1024)} %plus_hbm.1, s32[1152]{0:T(1024)} %minus_hbm.1, s32[32,96]{1,0:T(8,128)} %bitcast.7, f32[1152,8]{1,0:T(8,128)} %constant.4.clone.table_hbm, ...), custom_call_target="tpu_custom_call" | custom-call | tf_op jit(solution)/shard_map/pallas_call | solution.py:736
  170.3 0.0 copy-start
  170.4 4.2 %copy.12 = f32[144,16,384]{2,1,0:T(8,128)} copy(f32[144,16,384]{2,1,0:T(8,128)} %get-tuple-element.8) | data formatting | bytes 7077888
  174.5 0.0 copy-done
  174.5 1.3 copy.13
Async XLA Ops:
  170.3 4.2 %copy-start = (f32[128,32,96]{2,1,0:T(8,128)S(1)}, f32[128,32,96]{2,1,0:T(8,128)}, u32[]{:S(2)}) copy-start(f32[128,32,96]{2,1,0:T(8,128)} %get-tuple-element.5) | copy-start | bytes 4718596

commit v3 on v2

--- a/solution.py
+++ b/solution.py
@@ -170,8 +170,14 @@
 LEAD = 2
 FORTH = ((0, 1, 5, 9), (0, 4, 9))
 HOME = ((0, 3, 6, 8, 9), (0, 3, 6, 9))
+LAST = 1
+PLANES = 2
 QUEUE = ((0, 0), (0, 1), (1, 0), (1, 1), (1, 2), (0, 2), (0, 3))
 AHEAD = 2
+
+
+def order(count):
+    return list(range(count // 2, count)) + list(range(1, count // 2)) + [0]
 F32 = jnp.float32
 
 
@@ -197,43 +203,44 @@
     return tiles
 
 
-def advect(get, wanted, coefs, face, half, mask):
-    cols = face.shape[1]
-    lane = lax.broadcasted_iota(jnp.int32, (8, cols), 1)
+def advect(get, wanted, coefs, face_ref, half_ref, mask_ref, put):
+    cols = face_ref.shape[1]
+    across = cols // TILE
+    lane = lax.broadcasted_iota(jnp.int32, (8, TILE), 1)
     at_first = lane == 0
     at_second = lane <= 1
-    at_last = lane == cols - 1
-    sixth = F32(1.0 / 6.0)
-    coef = [jnp.broadcast_to(coefs[:, i : i + 1], (8, cols)) for i in range(6)]
-    cache = {}
-
-    def f(row):
-        if row not in cache:
-            cache[row] = get(row)
-        return cache[row]
-
-    results = []
+    at_last = lane == TILE - 1
+    coef = [jnp.broadcast_to(coefs[:, i : i + 1], (8, TILE)) for i in range(6)]
     for row in wanted:
-        c = f(row)
-        m1 = jnp.where(at_first, 0.0, pltpu.roll(c, 1, 1))
-        m2 = jnp.where(at_second, 0.0, pltpu.roll(c, 2, 1))
-        p1 = jnp.where(at_last, 0.0, pltpu.roll(c, cols - 1, 1))
-        speed = coef[0] + face[row : row + 1, :]
-        ahead = speed > 0.0
-        part = 3.0 * jnp.where(ahead, m1, c) - jnp.where(ahead, m2, p1)
-        flux = (speed * sixth) * (part + 2.0 * (m1 + c))
-        end_speed = coef[0] + half[row : row + 1, :]
-        end = (end_speed * sixth) * jnp.where(end_speed > 0.0, 5.0 * c - m1, 2.0 * c)
-        upper = jnp.where(at_last, end, pltpu.roll(flux, cols - 1, 1))
-        along_y = (
-            coef[1] * f(row - 2)
-            + coef[2] * f(row - 1)
-            + coef[3] * c
-            + coef[4] * f(row + 1)
-            + coef[5] * f(row + 2)
-        )
-        results.append(mask[row : row + 1, :] * (c - ((upper - flux) + along_y)))
-    return results
+        c = [get(row, t) for t in range(across)]
+        one = [pltpu.roll(value, 1, 1) for value in c]
+        two = [pltpu.roll(value, 2, 1) for value in c]
+        back = [pltpu.roll(value, TILE - 1, 1) for value in c]
+        flux = []
+        for t in range(across):
+            lanes = slice(t * TILE, (t + 1) * TILE)
+            m1 = jnp.where(at_first, one[t - 1] if t else 0.0, one[t])
+            m2 = jnp.where(at_second, two[t - 1] if t else 0.0, two[t])
+            p1 = jnp.where(at_last, back[t + 1] if t + 1 < across else 0.0, back[t])
+            speed = coef[0] + face_ref[row : row + 1, lanes]
+            ahead = speed > 0.0
+            part = 3.0 * jnp.where(ahead, m1, c[t]) - jnp.where(ahead, m2, p1)
+            flux.append(speed * (part + 2.0 * (m1 + c[t])))
+            if t + 1 == across:
+                end_speed = coef[0] + half_ref[row : row + 1, lanes]
+                end = end_speed * jnp.where(end_speed > 0.0, 5.0 * c[t] - m1, 2.0 * c[t])
+        shifted = [pltpu.roll(value, TILE - 1, 1) for value in flux]
+        for t in range(across):
+            lanes = slice(t * TILE, (t + 1) * TILE)
+            upper = jnp.where(at_last, shifted[t + 1] if t + 1 < across else end, shifted[t])
+            along_y = (
+                coef[1] * get(row - 2, t)
+                + coef[2] * get(row - 1, t)
+                + coef[3] * c[t]
+                + coef[4] * get(row + 1, t)
+                + coef[5] * get(row + 2, t)
+            )
+            put(row, t, mask_ref[row : row + 1, lanes] * (c[t] - ((upper - flux[t]) + along_y)))
 
 
 def halves(value):
@@ -254,6 +261,11 @@
     drift_hbm,
     out_ref,
     stokes_ref,
+    rows_out,
+    low_out,
+    high_out,
+    fields_out,
+    coefs_out,
     block,
     by_row,
     leaving,
@@ -302,10 +314,12 @@
     near_recv,
     out_sem,
     ocean_sem,
+    rows_sem,
+    fields_sem,
 ):
     me = lax.axis_index("bins")
     band = lax.axis_index("lat")
-    local, rows, cols = block.shape
+    rows, local, cols = by_row.shape
     bins = local * count
     strip = cols // count
     each = strip // LANES
@@ -333,9 +347,11 @@
 
     chunk_load = local // LOADS
 
-    def load_copy(part):
-        here = pl.ds(part * chunk_load, chunk_load)
-        return pltpu.make_async_copy(x_ref.at[here], block.at[here], load_sem.at[part])
+    def load_copy(part, t):
+        here = pl.ds(part * chunk_load * rows, chunk_load * rows)
+        return pltpu.make_async_copy(
+            x_ref.at[here, pl.ds(t * TILE, TILE)], block.at[t, here, :], load_sem.at[part, t]
+        )
 
     first_bin = me * local
     own_bins = pl.ds(pl.multiple_of(first_bin, 8), local)
@@ -357,7 +373,8 @@
     for copy in table_copies[:2]:
         copy.start()
     for part in range(LOADS):
-        load_copy(part).start()
+        for t in range(across):
+            load_copy(part, t).start()
 
     near[...] = jnp.zeros_like(near)
     barrier = pltpu.get_barrier_semaphore()
@@ -390,13 +407,17 @@
         strip_copy(step).start()
 
     for part in range(LOADS):
-        load_copy(part).wait()
+        for t in range(across):
+            load_copy(part, t).wait()
 
         def turn_step(i, carry, part=part):
             here = pl.ds(pl.multiple_of(part * chunk_load + i * 8, 8), 8)
-            turned = pltpu.einshape("brl->rbl", block[here, :, :] * mask[...][None])
+            start = (part * chunk_load + i * 8) * rows
             for row in range(rows):
-                by_row[row, here, :] = turned[row]
+                there = pl.ds(start + row, 8, stride=rows)
+                for t in range(across):
+                    lanes = slice(t * TILE, (t + 1) * TILE)
+                    by_row[row, here, lanes] = block[t, there, :] * mask[row : row + 1, lanes]
             return carry
 
         lax.fori_loop(0, chunk_load // 8, turn_step, 0)
@@ -419,28 +440,50 @@
     for peer in range(count):
         piece = jnp.concatenate([strips[peer], rest], axis=1)
         spread = spread + (pltpu.roll(piece, peer * strip, 1) if peer else piece)
+    spread = spread * F32(1.0 / 6.0)
     half[...] = spread
     first_lane = lax.broadcasted_iota(jnp.int32, (rows, cols), 1) == 0
     face[...] = spread + jnp.where(first_lane, 0.0, pltpu.roll(spread, 1, 1))
+    field_copies = [
+        pltpu.make_async_copy(src, dst, fields_sem.at[i])
+        for i, (src, dst) in enumerate(
+            (
+                (face, fields_out.at[0]),
+                (half, fields_out.at[1]),
+                (mask, fields_out.at[2]),
+                (coefs, coefs_out),
+            )
+        )
+    ]
 
     def fetch(here, low, high):
-        def get(row):
+        def get(row, t):
+            lanes = slice(t * TILE, (t + 1) * TILE)
             if row < 0:
-                return edges[0] * low[row + 2, here, :]
+                return edges[0] * low[row + 2, here, lanes]
             if row >= rows:
-                return edges[1] * high[row - rows, here, :]
-            return by_row[row, here, :]
+                return edges[1] * high[row - rows, here, lanes]
+            return by_row[row, here, lanes]
 
         return get
 
     def coefs_at(start):
         return coefs[pl.ds(pl.multiple_of(start, 8), 8), :]
 
+    def flip(step):
+        peer = me
+        weight = 1
+        while weight < count:
+            if step & weight:
+                peer = peer + weight - 2 * weight * lax.rem(me // weight, 2)
+            weight *= 2
+        return peer
+
     def reach(cuts, part):
         return cuts[part] * unit, (cuts[part + 1] - cuts[part]) * unit
 
     def in_copy(h, part, step):
-        peer = lax.rem(me + step, count)
+        peer = flip(step)
         at, size = reach(FORTH[h], part)
         src = leaving.at[h, pl.ds(peer * each, each), pl.ds(at, size), :]
         dst = arrived.at[h, :, pl.ds(pl.multiple_of(first_bin + at, 8), size), :]
@@ -457,16 +500,18 @@
             def forth_step(i, carry):
                 start = turn * unit + i * 8
                 here = pl.ds(pl.multiple_of(start, 8), 8)
-                found = advect(
+                found = {}
+                advect(
                     fetch(here, low_halo, high_halo),
                     groups[h],
                     coefs_at(start),
-                    face[...],
-                    half[...],
-                    mask[...],
+                    face,
+                    half,
+                    mask,
+                    lambda row, t, value: found.update({(row, t): value}),
                 )
                 for t in range(across):
-                    turned = turn_blocks([row[:, t * TILE : (t + 1) * TILE] for row in found])
+                    turned = turn_blocks([found[row, t] for row in groups[h]])
                     for q in range(GROUP):
                         leaving[h, t * GROUP + q, here, :] = turned[q]
                 return carry
@@ -476,8 +521,8 @@
 
                 @pl.when(turn == end - 1)
                 def _(part=part):
-                    for step in range(1, count + 1):
-                        in_copy(h, part, step % count).start()
+                    for step in order(count):
+                        in_copy(h, part, step).start()
 
             return carry
 
@@ -499,12 +544,14 @@
         back_table[here, :] = back.astype(jnp.bfloat16)
         return carry
 
+    for copy in field_copies:
+        copy.start()
     for copy in table_copies[3:]:
         copy.wait()
     lax.fori_loop(0, tiles, table_step, 0)
 
     def back_copy(h, part, step):
-        peer = lax.rem(me + step, count)
+        peer = flip(step)
         at, size = reach(HOME[h], part)
         src = middle.at[h, :, pl.ds(pl.multiple_of(peer * local + at, 8), size), :]
         dst = returned.at[h, pl.ds(me * each, each), pl.ds(at, size), :]
@@ -513,8 +560,8 @@
         return remote(src, dst, back_send.at[h, part, step], back_recv.at[h, part, step], peer)
 
     def send_back(at):
-        for step in range(1, count + 1):
-            back_copy(*QUEUE[at], step % count).start()
+        for step in order(count):
+            back_copy(*QUEUE[at], step).start()
 
     def await_back(at):
         for step in range(count):
@@ -658,9 +705,18 @@
             src, dst, peer = by_row.at[pl.ds(rows - 2, 2), here, :], low_again.at[:, here, :], above
         return remote(src, dst, again_send.at[slot, part], again_recv.at[slot, part], peer, "lat")
 
-    def out_copy(part):
-        here = pl.ds(part * unit, unit)
-        return pltpu.make_async_copy(block.at[here], out_ref.at[here], out_sem.at[part])
+    def out_copy(part, t):
+        here = pl.ds(pl.multiple_of(part * unit * rows, 8), unit * rows)
+        return pltpu.make_async_copy(
+            block.at[t, here, :], out_ref.at[here, pl.ds(t * TILE, TILE)], out_sem.at[part, t]
+        )
+
+    def rows_copy(at, which):
+        here = pl.ds(pl.multiple_of((STEPS - LAST + at) * unit, 8), unit)
+        there = pl.ds(pl.multiple_of(at * unit, 8), unit)
+        src = (by_row, low_again, high_again)[which]
+        dst = (rows_out, low_out, high_out)[which]
+        return pltpu.make_async_copy(src.at[:, here, :], dst.at[:, there, :], rows_sem.at[at, which])
 
     def unpack(h, turn):
         for at, (which, part) in enumerate(QUEUE):
@@ -681,12 +737,6 @@
         lax.fori_loop(0, unit // 8, unpack_step, 0)
 
     def home_part(turn, carry):
-        @pl.when(turn < STEPS)
-        def _():
-            unpack(1, turn)
-            again_copy(turn, 0).start()
-            again_copy(turn, 1).start()
-
         @pl.when(turn >= LEAD)
         def _():
             part = turn - LEAD
@@ -694,31 +744,209 @@
             again_copy(part, 0).wait()
             again_copy(part, 1).wait()
 
-            def home_step(i, carry):
-                start = part * unit + i * 8
-                here = pl.ds(pl.multiple_of(start, 8), 8)
-                found = advect(
-                    fetch(here, low_again, high_again),
-                    list(range(rows)),
-                    coefs_at(start),
-                    face[...],
-                    half[...],
-                    mask[...],
-                )
-                block[here, :, :] = pltpu.einshape("rbl->brl", jnp.stack(found))
-                return carry
-
-            lax.fori_loop(0, unit // 8, home_step, 0)
-            out_copy(part).start()
+            @pl.when(part < STEPS - LAST)
+            def _():
+                def home_step(i, carry):
+                    start = part * unit + i * 8
+                    here = pl.ds(pl.multiple_of(start, 8), 8)
+
+                    def put(row, t, value):
+                        there = pl.ds(start * rows + row, 8, stride=rows)
+                        block[t, there, :] = value
+
+                    advect(
+                        fetch(here, low_again, high_again),
+                        list(range(rows)),
+                        coefs_at(start),
+                        face,
+                        half,
+                        mask,
+                        put,
+                    )
+                    return carry
+
+                lax.fori_loop(0, unit // 8, home_step, 0)
+                for t in range(across):
+                    out_copy(part, t).start()
+
+            @pl.when(part >= STEPS - LAST)
+            def _():
+                for which in range(3):
+                    rows_copy(part - (STEPS - LAST), which).start()
+
+        @pl.when(turn < STEPS)
+        def _():
+            unpack(1, turn)
+            again_copy(turn, 0).start()
+            again_copy(turn, 1).start()
 
         return carry
 
     await_back(1)
     lax.fori_loop(0, STEPS + LEAD, home_part, 0)
-    for part in range(STEPS):
-        out_copy(part).wait()
+    for part in range(STEPS - LAST):
+        for t in range(across):
+            out_copy(part, t).wait()
+    for at in range(LAST):
+        for which in range(3):
+            rows_copy(at, which).wait()
+    for copy in field_copies:
+        copy.wait()
     for copy in ocean_copies:
         copy.wait()
+
+
+def settle_kernel(
+    second_ref,
+    stokes_ref,
+    rows_ref,
+    low_ref,
+    high_ref,
+    fields_ref,
+    coefs_ref,
+    second_out,
+    stokes_out,
+    held,
+    planes,
+    by_row,
+    low,
+    high,
+    fields,
+    coefs,
+    done,
+    first_sem,
+    load_sem,
+    store_sem,
+    plane_load,
+    plane_store,
+    done_sem,
+):
+    band = lax.axis_index("lat")
+    bands = lax.axis_size("lat")
+    edges = (jnp.where(band > 0, F32(1.0), F32(0.0)), jnp.where(band < bands - 1, F32(1.0), F32(0.0)))
+    rows, tail, cols = by_row.shape
+    across = cols // TILE
+    start = held.shape[0] // rows
+    turns = tail // 8
+    size = held.shape[0] // turns
+    depth = planes.shape[0] // PLANES
+    firsts = [
+        pltpu.make_async_copy(src, dst, first_sem.at[i])
+        for i, (src, dst) in enumerate(
+            (
+                (fields_ref, fields),
+                (coefs_ref, coefs),
+                (low_ref, low),
+                (high_ref, high),
+                (rows_ref, by_row),
+            )
+        )
+    ]
+
+    def held_load(i):
+        here = pl.ds(pl.multiple_of(i * size, 8), size)
+        return pltpu.make_async_copy(second_ref.at[here], held.at[here], load_sem.at[i])
+
+    def held_store(i):
+        here = pl.ds(pl.multiple_of(i * size, 8), size)
+        return pltpu.make_async_copy(held.at[here], second_out.at[here], store_sem.at[i])
+
+    def plane_in(i):
+        here = pl.ds(i * depth, depth)
+        return pltpu.make_async_copy(stokes_ref.at[here], planes.at[here], plane_load.at[i])
+
+    def plane_back(i):
+        here = pl.ds(i * depth, depth)
+        return pltpu.make_async_copy(planes.at[here], stokes_out.at[here], plane_store.at[i])
+
+    def done_store(i, t):
+        src = pl.ds(pl.multiple_of(i * 8 * rows, 8), 8 * rows)
+        dst = pl.ds(pl.multiple_of((start + i * 8) * rows, 8), 8 * rows)
+        return pltpu.make_async_copy(
+            done.at[t, src, :], second_out.at[dst, pl.ds(t * TILE, TILE)], done_sem.at[i, t]
+        )
+
+    for copy in firsts:
+        copy.start()
+    for i in range(turns):
+        held_load(i).start()
+    for i in range(PLANES):
+        plane_in(i).start()
+    for copy in firsts:
+        copy.wait()
+
+    def turn_step(i, carry):
+        held_load(i).wait()
+        held_store(i).start()
+        here = pl.ds(pl.multiple_of(i * 8, 8), 8)
+
+        def get(row, t):
+            lanes = slice(t * TILE, (t + 1) * TILE)
+            if row < 0:
+                return edges[0] * low[row + 2, here, lanes]
+            if row >= rows:
+                return edges[1] * high[row - rows, here, lanes]
+            return by_row[row, here, lanes]
+
+        def put(row, t, value):
+            done[t, pl.ds(i * 8 * rows + row, 8, stride=rows), :] = value
+
+        advect(
+            get,
+            list(range(rows)),
+            coefs[pl.ds(pl.multiple_of(start + i * 8, 8), 8), :],
+            fields.at[0],
+            fields.at[1],
+            fields.at[2],
+            put,
+        )
+        for t in range(across):
+            done_store(i, t).start()
+        plane_in(i).wait()
+        plane_back(i).start()
+        return carry
+
+    lax.fori_loop(0, turns, turn_step, 0)
+    for i in range(turns):
+        held_store(i).wait()
+        for t in range(across):
+            done_store(i, t).wait()
+    for i in range(PLANES):
+        plane_back(i).wait()
+
+
+def settle(second, stokes, by_row, low, high, fields, coefs):
+    hbm = pl.BlockSpec(memory_space=pl.ANY)
+    dma = pltpu.SemaphoreType.DMA
+    rows, tail, cols = by_row.shape
+    turns = tail // 8
+    across = cols // TILE
+    return pl.pallas_call(
+        settle_kernel,
+        out_shape=(
+            jax.ShapeDtypeStruct(second.shape, F32),
+            jax.ShapeDtypeStruct(stokes.shape, F32),
+        ),
+        in_specs=[hbm] * 7,
+        out_specs=(hbm, hbm),
+        scratch_shapes=[
+            VMEM((second.shape[0] - tail * rows, cols), F32),
+            VMEM(stokes.shape, F32),
+            VMEM(by_row.shape, F32),
+            VMEM(low.shape, F32),
+            VMEM(high.shape, F32),
+            VMEM(fields.shape, F32),
+            VMEM(coefs.shape, F32),
+            VMEM((across, tail * rows, TILE), F32),
+            dma((5,)),
+            dma((turns,)),
+            dma((turns,)),
+            dma((PLANES,)),
+            dma((PLANES,)),
+            dma((turns, across)),
+        ],
+        compiler_params=pltpu.CompilerParams(vmem_limit_bytes=58 * 1024 * 1024),
+    )(second, stokes, by_row, low, high, fields, coefs)
 
 
 def step_call(spectrum, sea_mask, current, plus, minus, source_map, coefs, drift_table, count, bands):
@@ -729,6 +957,7 @@
     strip = cols // count
     each = strip // LANES
     pieces = cols // LANES
+    tail = local // STEPS * LAST
     hbm = pl.BlockSpec(memory_space=pl.ANY)
     dma = pltpu.SemaphoreType.DMA
     forth = max(len(cuts) for cuts in FORTH) - 1
@@ -736,13 +965,18 @@
     return pl.pallas_call(
         functools.partial(step_kernel, count, bands),
         out_shape=(
-            jax.ShapeDtypeStruct(spectrum.shape, F32),
+            jax.ShapeDtypeStruct((local * rows, cols), F32),
             jax.ShapeDtypeStruct((profiles, lats, lons), F32),
+            jax.ShapeDtypeStruct((rows, tail, cols), F32),
+            jax.ShapeDtypeStruct((2, tail, cols), F32),
+            jax.ShapeDtypeStruct((2, tail, cols), F32),
+            jax.ShapeDtypeStruct((3, rows, cols), F32),
+            jax.ShapeDtypeStruct((local, coefs.shape[1]), F32),
         ),
         in_specs=[pl.BlockSpec(memory_space=pltpu.HBM)] * 8,
-        out_specs=(hbm, hbm),
+        out_specs=(hbm,) * 7,
         scratch_shapes=[
-            VMEM((local, rows, cols), F32),
+            VMEM((cols // TILE, local * rows, TILE), F32),
             VMEM((rows, local, cols), F32),
             VMEM((2, pieces, local, TILE), F32),
             VMEM((2, each, bins, TILE), F32),
@@ -774,7 +1008,7 @@
             VMEM(plus.shape, jnp.int32),
             VMEM(minus.shape, jnp.int32),
             VMEM(source_map.shape, jnp.int32),
-            dma((LOADS,)),
+            dma((LOADS, cols // TILE)),
             dma((8,)),
             dma((count,)),
             dma((count,)),
@@ -788,13 +1022,15 @@
             dma((2, STEPS)),
             dma((4,)),
             dma((4,)),
-            dma((STEPS,)),
+            dma((STEPS, cols // TILE)),
             dma((lats // 8,)),
+            dma((LAST, 3)),
+            dma((4,)),
         ],
         compiler_params=pltpu.CompilerParams(
             collective_id=0, has_side_effects=True, vmem_limit_bytes=58 * 1024 * 1024
         ),
-    )(spectrum, sea_mask, current, plus, minus, source_map, coefs, drift_table)
+    )(spectrum.reshape(local * rows, cols), sea_mask, current, plus, minus, source_map, coefs, drift_table)
 
 
 def on_device_fast(spectrum, sea_mask, current, partner_plus, partner_minus, source_map):
@@ -805,7 +1041,7 @@
     back = np.minimum(along_y, 0.0) / 6.0
     coefs = np.stack(
         [
-            along_x,
+            along_x / 6.0,
             forth,
             -6.0 * forth - 2.0 * back,
             3.0 * forth - 3.0 * back,
@@ -816,7 +1052,7 @@
         ],
         axis=1,
     ).astype(np.float32)
-    second, stokes = step_call(
+    second, stokes = settle(*step_call(
         spectrum,
         sea_mask,
         current.T,
@@ -827,9 +1063,9 @@
         jnp.asarray(drift_table),
         count,
         bands,
-    )
+    ))
     lons, lats = source_map.shape
-    return (second, jnp.swapaxes(stokes.reshape(2, LEV, lats, lons), 2, 3))
+    return (second.reshape(spectrum.shape), jnp.swapaxes(stokes.reshape(2, LEV, lats, lons), 2, 3))
 
 
 def on_device(spectrum, sea_mask, current, partner_plus, partner_minus, source_map):
@@ -848,9 +1084,13 @@
         and strip <= TILE
         and bins * count % TILE == 0
         and lats == 2 * rows
+        and 2 * LEV % PLANES == 0
+        and (STEPS - LAST) * rows % LAST == 0
+        and PLANES == LAST * bins // (8 * STEPS)
         and lons == 2 * strip
         and lons <= TILE
         and count > 2
+        and count & (count - 1) == 0
         and bands > 2
     )
     body = on_device_fast if fits else on_device_plain

time: 178 us -> 176 us (0.989)
  local copies, waits for them, and re-layouts: 5.49 us -> 0 us
  Pallas kernels: 170 us -> 175 us
    unnamed x4 -> x0, local copies, waits for them, and re-layouts: 5.49 us -> none
    pallas_call x0 -> x1, Pallas kernels: none -> 4.73 us  [settle(): pl.pallas_call(settle_kernel, out_shape=(jax.ShapeDtypeStruct(second.shap...]
where the time goes in v3:
time: 176 us
  Pallas kernels  175 us (99%)
    pallas_call x1, Pallas kernels, step_call(): pl.pallas_call(functools.partial(step_kernel, count, bands), out_shape=(j...  170 us
    pallas_call x1, Pallas kernels, settle(): pl.pallas_call(settle_kernel, out_shape=(jax.ShapeDtypeStruct(second.shap...  4.73 us

profile of v3, /device:TPU:9, one launch (start us, length us, event | category | flops | bytes accessed | tf_op | source)
XLA Modules:
  0.0 175.5 jit_solution(3519785689987312912)
XLA Ops:
  0.6 170.2 %shard_map.95 = (f32[2304,384]{1,0:T(8,128)}, f32[128,32,96]{2,1,0:T(8,128)}, f32[16,16,384]{2,1,0:T(8,128)}, f32[2,16,384]{2,1,0:T(8,128)}, f32[2,16,384]{2,1,0...) custom-call(f32[2304,384]{1,0:T(8,128)} %bitcast.7, s32[16,384]{1,0:T(8,128)} %mask_hbm.1, f32[32,96]{1,0:T(8,128)} %bitcast.8, ...), custom_call_target="tpu_custom_call" | custom-call | tf_op jit(solution)/shard_map/pallas_call | solution.py:965
  170.8 4.7 %shard_map.96 = (f32[2304,384]{1,0:T(8,128)}, f32[128,32,96]{2,1,0:T(8,128)}) custom-call(f32[2304,384]{1,0:T(8,128)} %get-tuple-element.11.second_ref, f32[128,32,96]{2,1,0:T(8,128)} %get-tuple-element.12.stokes_ref, f32[16,16,384]{2,1,0:T(8,128)} %get-tuple-element.13.rows_ref, f32[2,16,384]{2,1,0:T(8,128)} %get-tuple-element.14.low_ref, ...), custom_call_target="tpu_custom_call" | custom-call | tf_op jit(solution)/shard_map/pallas_call | solution.py:924

commit v4 on v3

--- a/solution.py
+++ b/solution.py
@@ -171,6 +171,7 @@
 FORTH = ((0, 1, 5, 9), (0, 4, 9))
 HOME = ((0, 3, 6, 8, 9), (0, 3, 6, 9))
 LAST = 1
+CUTS = 4
 PLANES = 2
 QUEUE = ((0, 0), (0, 1), (1, 0), (1, 1), (1, 2), (0, 2), (0, 3))
 AHEAD = 2
@@ -828,7 +829,7 @@
     across = cols // TILE
     start = held.shape[0] // rows
     turns = tail // 8
-    size = held.shape[0] // turns
+    size = held.shape[0] // (turns * CUTS)
     depth = planes.shape[0] // PLANES
     firsts = [
         pltpu.make_async_copy(src, dst, first_sem.at[i])
@@ -868,7 +869,7 @@
 
     for copy in firsts:
         copy.start()
-    for i in range(turns):
+    for i in range(turns * CUTS):
         held_load(i).start()
     for i in range(PLANES):
         plane_in(i).start()
@@ -876,8 +877,9 @@
         copy.wait()
 
     def turn_step(i, carry):
-        held_load(i).wait()
-        held_store(i).start()
+        for cut in range(CUTS):
+            held_load(i * CUTS + cut).wait()
+            held_store(i * CUTS + cut).start()
         here = pl.ds(pl.multiple_of(i * 8, 8), 8)
 
         def get(row, t):
@@ -907,8 +909,9 @@
         return carry
 
     lax.fori_loop(0, turns, turn_step, 0)
+    for i in range(turns * CUTS):
+        held_store(i).wait()
     for i in range(turns):
-        held_store(i).wait()
         for t in range(across):
             done_store(i, t).wait()
     for i in range(PLANES):
@@ -939,8 +942,8 @@
             VMEM(coefs.shape, F32),
             VMEM((across, tail * rows, TILE), F32),
             dma((5,)),
-            dma((turns,)),
-            dma((turns,)),
+            dma((turns * CUTS,)),
+            dma((turns * CUTS,)),
             dma((PLANES,)),
             dma((PLANES,)),
             dma((turns, across)),
@@ -1085,7 +1088,7 @@
         and bins * count % TILE == 0
         and lats == 2 * rows
         and 2 * LEV % PLANES == 0
-        and (STEPS - LAST) * rows % LAST == 0
+        and (STEPS - LAST) * rows % (LAST * CUTS) == 0
         and PLANES == LAST * bins // (8 * STEPS)
         and lons == 2 * strip
         and lons <= TILE

time: 176 us -> 176 us (level)
  no operation moved by 1% of the time
where the time goes in v4:
time: 176 us
  Pallas kernels  175 us (99%)
    pallas_call x1, Pallas kernels, step_call(): pl.pallas_call(functools.partial(step_kernel, count, bands), out_shape=(j...  170 us
    pallas_call x1, Pallas kernels, settle(): pl.pallas_call(settle_kernel, out_shape=(jax.ShapeDtypeStruct(second.shap...  5.14 us

profile of v4, /device:TPU:9, one launch (start us, length us, event | category | flops | bytes accessed | tf_op | source)
XLA Modules:
  0.0 175.9 jit_solution(6711951612803979482)
XLA Ops:
  0.6 170.2 %shard_map.95 = (f32[2304,384]{1,0:T(8,128)}, f32[128,32,96]{2,1,0:T(8,128)}, f32[16,16,384]{2,1,0:T(8,128)}, f32[2,16,384]{2,1,0:T(8,128)}, f32[2,16,384]{2,1,0...) custom-call(f32[2304,384]{1,0:T(8,128)} %bitcast.7, s32[16,384]{1,0:T(8,128)} %mask_hbm.1, f32[32,96]{1,0:T(8,128)} %bitcast.8, ...), custom_call_target="tpu_custom_call" | custom-call | tf_op jit(solution)/shard_map/pallas_call | solution.py:968
  170.8 5.1 %shard_map.96 = (f32[2304,384]{1,0:T(8,128)}, f32[128,32,96]{2,1,0:T(8,128)}) custom-call(f32[2304,384]{1,0:T(8,128)} %get-tuple-element.11.second_ref, f32[128,32,96]{2,1,0:T(8,128)} %get-tuple-element.12.stokes_ref, f32[16,16,384]{2,1,0:T(8,128)} %get-tuple-element.13.rows_ref, f32[2,16,384]{2,1,0:T(8,128)} %get-tuple-element.14.low_ref, ...), custom_call_target="tpu_custom_call" | custom-call | tf_op jit(solution)/shard_map/pallas_call | solution.py:927
